TPU v7x, 256 devices: a whole 4x4x8 slice. The times are simulated.
256 devices in a mesh: grp: 32 (over z, x), nbr: 8 (over y, core).
Axes of the slice: x: 4, y: 4, z: 8, core: 2. Of those that a mesh axis runs over, the one named last changes fastest.
Arguments:
- gains: float32 [1024, 256, 256], P(('grp', 'nbr')), may hold values from -1 to 1
- covs: float32 [1024, 256, 256], P(('grp', 'nbr')), may hold values from -10 to 10, as said below
- terminal: float32 [256, 256], replicated, may hold values from -4 to 4, as said below
Outputs:
- smoothed: float32 [1024, 256, 256], P(('grp', 'nbr'))
Inputs may be any that keep to these rules, and one draw needn't show every extreme that they name: `covs`: each matrix is symmetric positive definite. `terminal`: symmetric positive definite.
All inputs are finite; a program needn't handle non-finite values.
Results may differ from a plain program's by a relative error of at most 0.0003.
Values sent between devices are 32-bit elements; how exact they have to be, the bound alone decides.
No kernel may reach another device: no remote copies, remote signals or barrier semaphores. Data moves between devices by JAX's collectives and lax.ppermute only.
A program may use at most 64 MiB of HBM per device.

v0:
```python
import jax
import jax.numpy as jnp
from jax import lax
from jax.sharding import PartitionSpec as P


def entering(x, axis, combine, identity):
    length, place = (lax.axis_size(axis), lax.axis_index(axis))
    everything = jax.tree.map(lambda part: lax.all_gather(part, axis), x)
    start = jax.tree.map(
        lambda part, zero: jnp.broadcast_to(jnp.asarray(zero, part.dtype), part.shape), x, identity
    )

    def step(k, before):
        at = length - 1 - k
        reached = at > place
        new = combine(before, jax.tree.map(lambda part: part[at], everything))
        return jax.tree.map(lambda a, b: jnp.where(reached, a, b), new, before)

    return lax.fori_loop(0, length, step, start)


def broadcast(x, axis, root):
    mine = lax.axis_index(axis) == root
    return lax.psum(jnp.where(mine, x, jnp.zeros_like(x)), axis)


def matmul(left, right):
    return jnp.matmul(
        left, right, precision=lax.Precision.HIGHEST, preferred_element_type=jnp.float32
    )


def matmul_tr(left, right):
    return jnp.matmul(
        left,
        jnp.swapaxes(right, -1, -2),
        precision=lax.Precision.HIGHEST,
        preferred_element_type=jnp.float32,
    )


def compose(first, second):
    gain_a, cov_a = first
    gain_b, cov_b = second
    mixed = matmul(gain_a, cov_b)
    return (matmul(gain_a, gain_b), matmul_tr(mixed, gain_a) + cov_a)


def combine(earlier, later):
    return compose(later, earlier)


def per_device(gains, covs, terminal):
    count = gains.shape[0]
    width = gains.shape[1]
    identity = (jnp.eye(width, dtype=jnp.float32), jnp.zeros((width, width), jnp.float32))
    total = (gains[count - 1], covs[count - 1])
    for step in range(count - 2, -1, -1):
        total = compose((gains[step], covs[step]), total)
    after = entering(total, "nbr", combine, identity)
    inclusive = compose(total, after)
    group_total = (broadcast(inclusive[0], "nbr", 0), broadcast(inclusive[1], "nbr", 0))
    beyond = entering(group_total, "grp", combine, identity)
    suffix = compose(after, beyond)
    state = matmul_tr(matmul(suffix[0], terminal), suffix[0]) + suffix[1]
    results = []
    for step in range(count - 1, -1, -1):
        state = matmul_tr(matmul(gains[step], state), gains[step]) + covs[step]
        results.append(state)
    return jnp.stack(results[::-1], axis=0)


def solution(mesh):
    placed = (P(("grp", "nbr"), None, None), P(("grp", "nbr"), None, None), P())
    return jax.shard_map(
        per_device,
        mesh=mesh,
        in_specs=placed,
        out_specs=P(("grp", "nbr"), None, None),
        check_vma=False,
    )
```

profile of v0, /device:TPU:1, one launch (start us, length us, event | category | flops | bytes accessed | tf_op | source)
XLA Modules:
  0.0 525.8 jit_solution(11653446207569462237)
XLA Ops:
  6.5 1.6 fusion.56
  8.1 1.5 fusion.51
  9.7 2.1 fusion.43
  15.9 28.0 %all-gather.11.cloned.1.call-done = f32[2048,256]{0,1:T(8,128)} async-done(((f32[256,256]{0,1:T(8,128)}), f32[2048,256]{0,1:T(8,128)}) %all-gather.11.cloned.1.call-update) | async-done | bytes 2097168 | tf_op jit(solution)/shard_map/all_gather | solution.py:9
  43.9 2.9 copy.6
  46.8 27.0 %all-gather.13.cloned.1.call-done = f32[2048,256]{1,0:T(8,128)} async-done(((f32[256,256]{1,0:T(8,128)}), f32[2048,256]{1,0:T(8,128)}) %all-gather.13.cloned.1.call-update) | async-done | bytes 2097168 | tf_op jit(solution)/shard_map/all_gather | solution.py:9
  73.8 33.9 %while.36 = (s32[]{:T(128)}, f32[256,256]{1,0:T(8,128)S(1)}, f32[256,256]{1,0:T(8,128)S(1)}, s32[]{:T(128)}, f32[8,256,256]{2,1,0:T(8,128)}, /*index=5*/f32[8,25...) while((s32[]{:T(128)}, f32[256,256]{1,0:T(8,128)S(1)}, f32[256,256]{1,0:T(8,128)S(1)}, ...), condition=%wide.region_1.2_spmd.clone, body=%wide.region_0.1_spmd.clone.sunk | while | flops 604307456 | bytes 3672247 | solution.py:20
  76.6 1.5 fusion.147
  80.8 1.5 fusion.147
  85.0 1.5 fusion.147
  108.3 2.1 fusion.33
  111.8 63.9 %all-reduce.3.cloned.1.call-done = (f32[1,256,256]{2,1,0:T(8,128)}, f32[1,256,256]{2,1,0:T(8,128)}) async-done(((f32[1,256,256]{2,1,0:T(8,128)}, f32[1,256,256]{2,1,0:T(8,128)}), (f32[1,256,256]{2,1,0:T(8,128)}, f32[1,256,256]{2,1,0:T(8,128)})) %all-reduce.3.cloned.1.call-update) | async-done | bytes 524304 | tf_op jit(solution)/shard_map/psum | solution.py:25
  176.3 101.3 %all-gather.7.cloned.1.call-done = f32[32,256,256]{2,1,0:T(8,128)} async-done(((f32[1,256,256]{2,1,0:T(8,128)}), f32[32,256,256]{2,1,0:T(8,128)}) %all-gather.7.cloned.1.call-update) | async-done | bytes 8388624 | tf_op jit(solution)/shard_map/all_gather | solution.py:9
  277.6 98.2 %all-gather.9.cloned.1.call-done = f32[32,256,256]{2,1,0:T(8,128)} async-done(((f32[1,256,256]{2,1,0:T(8,128)}), f32[32,256,256]{2,1,0:T(8,128)}) %all-gather.9.cloned.1.call-update) | async-done | bytes 8388624 | tf_op jit(solution)/shard_map/all_gather | solution.py:9
  375.9 135.5 %while.37 = (s32[]{:T(128)}, f32[256,256]{1,0:T(8,128)S(1)}, f32[256,256]{1,0:T(8,128)S(1)}, s32[]{:T(128)}, f32[32,256,256]{2,1,0:T(8,128)}, /*index=5*/f32[32,...) while((s32[]{:T(128)}, f32[256,256]{1,0:T(8,128)S(1)}, f32[256,256]{1,0:T(8,128)S(1)}, ...), condition=%wide.region_5.6_spmd.clone, body=%wide.region_4.5_spmd.clone.sunk | while | flops 604307456 | bytes 3672247 | solution.py:20
  378.6 1.5 fusion.155
  382.8 1.5 fusion.155
  391.3 1.5 fusion.155
  399.8 1.5 fusion.155
  408.2 1.5 fusion.155
  416.7 1.5 fusion.155
  425.2 1.5 fusion.155
  433.6 1.5 fusion.155
  442.1 1.5 fusion.155
  450.6 1.5 fusion.155
  459.1 1.5 fusion.155
  467.5 1.5 fusion.155
  476.0 1.5 fusion.155
  484.5 1.5 fusion.155
  492.9 1.5 fusion.155
  501.4 1.5 fusion.155
  509.9 1.5 fusion.155
  (184 shorter events, 151.8 us)
Async XLA Ops:
  6.5 505.6 %copy-start = (f32[256,256]{1,0:T(8,128)S(1)}, f32[256,256]{1,0:T(8,128)}, u32[]{:S(2)}) copy-start(f32[256,256]{1,0:T(8,128)} %param.9) | copy-start | bytes 786436
  6.5 5.3 %copy-start.1 = (f32[4,256,256]{2,1,0:T(8,128)S(1)}, f32[4,256,256]{2,1,0:T(8,128)}, u32[]{:S(2)}) copy-start(f32[4,256,256]{2,1,0:T(8,128)} %param.7) | copy-start | bytes 3145732
  6.5 5.3 %copy-start.3 = (f32[4,256,256]{2,1,0:T(8,128)S(1)}, f32[4,256,256]{2,1,0:T(8,128)}, u32[]{:S(2)}) copy-start(f32[4,256,256]{2,1,0:T(8,128)} %param.8) | copy-start | bytes 3145732
  6.5 37.3 %all-gather.11.cloned.1.call-start = ((), (), s32[]{:S(2)}) async-start(), calls=%async_computation.2 | async-start | bytes 2359296 | tf_op jit(solution)/shard_map/all_gather | solution.py:9
  11.8 62.0 %all-gather.13.cloned.1.call-start = ((), (), s32[]{:S(2)}) async-start(), calls=%async_computation.3 | async-start | bytes 2359296 | tf_op jit(solution)/shard_map/all_gather | solution.py:9
  15.8 159.9 %all-reduce.3.cloned.1.call-start = ((), (), s32[]{:S(2)}) async-start(), calls=%async_computation.4 | async-start | bytes 1048576 | tf_op jit(solution)/shard_map/psum | solution.py:25
  73.8 33.9 %copy-start.2 = (f32[256,256]{1,0:T(8,128)S(1)}, f32[256,256]{1,0:T(8,128)}, u32[]{:S(2)}) copy-start(f32[256,256]{1,0:T(8,128)} %fusion.43) | copy-start | bytes 786436
  111.7 165.9 %all-gather.7.cloned.1.call-start = ((), (), s32[]{:S(2)}) async-start(), calls=%async_computation | async-start | bytes 8650752 | tf_op jit(solution)/shard_map/all_gather | solution.py:9
  175.7 200.2 %all-gather.9.cloned.1.call-start = ((), (), s32[]{:S(2)}) async-start(), calls=%async_computation.1 | async-start | bytes 8650752 | tf_op jit(solution)/shard_map/all_gather | solution.py:9
Sparse Core Ops, SparseCore 0:
  11.9 31.9 all-gather.10
  45.7 28.0 all-gather.12
  111.8 63.8 all-reduce.2
  178.5 99.1 all-gather.6
  280.4 95.4 all-gather.8
where the time goes:
time: 529 us; the launch traced here: 526 us
  waiting for transfers between devices  319 us (60%)
  matrix products  186 us (35%)
  between operations  13.4 us (3%)
    all_gather x4, waiting for transfers between devices, entering(): everything = jax.tree.map(lambda part: lax.all_gather(part, axis), x)  255 us
    dot_general x95, matrix products, matmul(): jnp.matmul(left, right, precision=lax.Precision.HIGHEST, preferred_elemen...  119 us
    dot_general x50, matrix products, matmul_tr(): jnp.matmul(left, jnp.swapaxes(right, -1, -2), precision=lax.Precision.HIG...  67.1 us
    psum x1, waiting for transfers between devices, broadcast(): return lax.psum(jnp.where(mine, x, jnp.zeros_like(x)), axis)  63.9 us
  transfers between devices with their start and end apart: 5, of which 5 were waited for; matrix products, arithmetic and copies ran while one was open for 1% of the time, Pallas kernels for 0%

commit v1 on v0

v1 whole, which is shorter than its diff:
```python
import jax
import jax.numpy as jnp
from jax import lax
from jax.experimental import pallas as pl
from jax.experimental.pallas import tpu as pltpu
from jax.sharding import PartitionSpec as P

AXES = ("grp", "nbr")
F32 = jnp.float32
BF16 = jnp.bfloat16


def split(a):
    high = a.astype(BF16)
    return high, (a - high.astype(F32)).astype(BF16)


def dot(a, b, transposed):
    dims = (((1,), (1 if transposed else 0,)), ((), ()))
    return lax.dot_general(a, b, dims, preferred_element_type=F32)


def product(a, b, transposed=False):
    (ah, al), (bh, bl) = a, b
    return dot(ah, bh, transposed) + (dot(ah, bl, transposed) + dot(al, bh, transposed))


def apply(gain, state):
    return product(split(product(gain, split(state))), gain, True)


def compose(first, second):
    gain = split(first[0])
    return product(gain, split(second[0])), apply(gain, second[1]) + first[1]


def pair_of(ref):
    return ref[0], ref[1]


def put(ref, pair):
    ref[0] = pair[0]
    ref[1] = pair[1]


def choose(flag, a, b):
    return jax.tree.map(lambda x, y: jnp.where(flag, x, y), a, b)


def other_pair(core, near, far):
    return choose(core == 0, (near, far), (far, near))


def local_kernel(gains, covs, total):
    pairs = [(gains[k], covs[k]) for k in range(gains.shape[0])]
    while len(pairs) > 1:
        pairs = [compose(*pairs[i : i + 2]) if i + 1 < len(pairs) else pairs[i] for i in range(0, len(pairs), 2)]
    put(total, pairs[0])


def merge(later, mine, other):
    return compose(choose(later, other, mine), choose(later, mine, other))


def outgoing(core, pair):
    return jnp.where(core == 0, pair[0], pair[1])


def first_kernel(flags, mine, other, total, send):
    new = merge(flags[1] != 0, pair_of(mine), pair_of(other))
    put(total, new)
    send[...] = outgoing(flags[0], new)


def total_kernel(flags, mine, near, far, total, send):
    other = other_pair(flags[0], near[...], far[...])
    new = merge(flags[1] != 0, pair_of(mine), other)
    put(total, new)
    send[...] = outgoing(flags[0], new)


def state_kernel(flags, mine, near, far, terminal, send):
    other = other_pair(flags[0], near[...], far[...])
    own = pair_of(mine)
    later = flags[1] != 0
    first, second = choose(later, other, own), choose(later, own, other)
    state = apply(split(second[0]), terminal[...]) + second[1]
    state = apply(split(first[0]), state) + first[1]
    half = send.shape[0]
    send[...] = jnp.where(flags[0] == 0, state[:half], state[half:])


def first_suffix_kernel(flags, other, suffix):
    later = flags[1] != 0
    size = suffix.shape[1]
    rows = lax.broadcasted_iota(jnp.int32, (size, size), 0)
    cols = lax.broadcasted_iota(jnp.int32, (size, size), 1)
    suffix[0] = jnp.where(later, (rows == cols).astype(F32), other[0])
    suffix[1] = jnp.where(later, jnp.zeros((size, size), F32), other[1])


def suffix_kernel(flags, before, near, far, suffix):
    old = pair_of(before)
    new = compose(old, other_pair(flags[0], near[...], far[...]))
    put(suffix, choose(flags[1] != 0, old, new))


def prepare_kernel(gains, covs, suffix, gain_out, cov_out):
    pair = pair_of(suffix)
    for k in range(gains.shape[0] - 1, -1, -1):
        pair = compose((gains[k], covs[k]), pair)
        gain_out[k] = pair[0]
        cov_out[k] = pair[1]


def final_kernel(flags, gains, covs, near, far, terminal, out):
    first = flags[0] == 0
    top, bottom = choose(first, (near[...], far[...]), (far[...], near[...]))
    state = jnp.where(flags[1] != 0, terminal[...], jnp.concatenate([top, bottom], axis=0))
    state = split(state)
    for k in range(gains.shape[0]):
        gain = split(gains[k])
        out[k] = product(split(product(gain, state)), gain, True) + covs[k]


def call(kernel, outs, products, flags, *args):
    vmem = pl.BlockSpec(memory_space=pltpu.VMEM)
    smem = [] if flags is None else [pl.BlockSpec(memory_space=pltpu.SMEM)]
    args = args if flags is None else (flags, *args)
    shapes = [jax.ShapeDtypeStruct(shape, F32) for shape in outs]
    width = outs[0][-1]
    return pl.pallas_call(
        kernel,
        out_shape=shapes,
        in_specs=smem + [vmem] * (len(args) - len(smem)),
        out_specs=[vmem] * len(shapes),
        cost_estimate=pl.CostEstimate(
            flops=products * 6 * width**3, transcendentals=0, bytes_accessed=4 * width * width * products
        ),
        compiler_params=pltpu.CompilerParams(vmem_limit_bytes=48 * 2**20),
    )(*args)


def per_device(gains, covs, terminal):
    count, width, _ = gains.shape
    groups, near_count = lax.axis_size("grp"), lax.axis_size("nbr")
    devices = groups * near_count
    place = lax.axis_index("grp") * near_count + lax.axis_index("nbr")
    core = place & 1
    levels = devices.bit_length() - 1
    matrix, pair = (width, width), (2, width, width)

    def flags(level):
        return jnp.stack([core, (place >> level) & 1]).astype(jnp.int32)

    def swap(x, distance):
        return lax.ppermute(x, AXES, [(i, i ^ distance) for i in range(devices)])

    (total,) = call(local_kernel, [pair], 9, None, gains, covs)
    other = swap(total, 1)
    total, send = call(first_kernel, [pair, matrix], 3, flags(0), total, other)
    (suffix,) = call(first_suffix_kernel, [pair], 1, flags(0), other)
    for level in range(1, levels - 1):
        near = swap(send, 1 << level)
        far = swap(near, 1)
        if level < levels - 2:
            total, send = call(total_kernel, [pair, matrix], 3, flags(level), total, near, far)
        else:
            (send,) = call(state_kernel, [(width // 2, width)], 4, flags(level), total, near, far, terminal)
        (suffix,) = call(suffix_kernel, [pair], 3, flags(level), suffix, near, far)
    half = devices // 2
    row = half // 4
    lower = []
    for i in range(half, devices):
        upper, rest = divmod(i - half, row)
        lower.append((i, (3 - upper) * row + rest))
    near = lax.ppermute(send, AXES, lower)
    far = swap(near, 1)
    ready, added = call(prepare_kernel, [(count, width, width)] * 2, 3 * count, None, gains, covs, suffix)
    (out,) = call(
        final_kernel, [(count, width, width)], 2 * count, flags(levels - 1), ready, added, near, far, terminal
    )
    return out


def solution(mesh):
    placed = (P(AXES, None, None), P(AXES, None, None), P())
    return jax.shard_map(
        per_device,
        mesh=mesh,
        in_specs=placed,
        out_specs=P(AXES, None, None),
        check_vma=False,
    )
```

time: 529 us -> 112 us (0.21)
  waiting for transfers between devices: 319 us -> 62.6 us
  matrix products: 186 us -> 0 us
  Pallas kernels: 0 us -> 25.7 us
  starting transfers between devices: 0.35 us -> 15.7 us
  between operations: 13.4 us -> 0.24 us
    all_gather x4 -> x0, waiting for transfers between devices: 255 us -> none  [entering(): everything = jax.tree.map(lambda part: lax.all_gather(part, axis), x)]
    dot_general x145 -> x0, matrix products: 186 us -> none  [the longest x95 119 us: matmul(): jnp.matmul(left, right, precision=lax.Precision.HIGHEST, preferred_elemen...]
    psum x1 -> x0, waiting for transfers between devices: 63.9 us -> none  [broadcast(): return lax.psum(jnp.where(mine, x, jnp.zeros_like(x)), axis)]
    ppermute x0 -> x15, waiting for transfers between devices: none -> 62.6 us  [the longest x14 58.9 us: swap(): return lax.ppermute(x, AXES, [(i, i ^ distance) for i in range(devices)])]
    pallas_call x0 -> x17, Pallas kernels: none -> 25.7 us  [call(): pl.pallas_call(kernel, out_shape=shapes, in_specs=smem + [vmem] * (len(ar...]
    ppermute x0 -> x15, starting transfers between devices: none -> 15.7 us  [the longest x14 14.4 us: swap(): return lax.ppermute(x, AXES, [(i, i ^ distance) for i in range(devices)])]
  transfers between devices with their start and end apart: 5 -> 15, of which waited for: 5 -> 14; matrix products, arithmetic and copies ran while one was open for 1% -> 1% of each run, Pallas kernels for 0% -> 10%
where the time goes in v1:
time: 112 us
  waiting for transfers between devices  62.6 us (56%)
  Pallas kernels  25.7 us (23%)
  starting transfers between devices  15.7 us (14%)
  local copies, waits for them, and re-layouts  6.91 us (6%)
    ppermute x14, waiting for transfers between devices, swap(): return lax.ppermute(x, AXES, [(i, i ^ distance) for i in range(devices)])  58.9 us
    pallas_call x17, Pallas kernels, call(): pl.pallas_call(kernel, out_shape=shapes, in_specs=smem + [vmem] * (len(ar...  25.7 us
    ppermute x14, starting transfers between devices, swap(): return lax.ppermute(x, AXES, [(i, i ^ distance) for i in range(devices)])  14.4 us
    unnamed x22, local copies, waits for them, and re-layouts  6.91 us
    ppermute x1, waiting for transfers between devices, per_device(): near = lax.ppermute(send, AXES, lower)  3.75 us
  transfers between devices with their start and end apart: 15, of which 14 were waited for; matrix products, arithmetic and copies ran while one was open for 1% of the time, Pallas kernels for 10%

profile of v1, /device:TPU:1, one launch (start us, length us, event | category | flops | bytes accessed | tf_op | source)
XLA Modules:
  0.0 111.7 jit_solution(15616302410477406348)
XLA Ops:
  0.0 1.2 %copy-done.1 = f32[4,256,256]{2,1,0:T(8,128)S(1)} copy-done((f32[4,256,256]{2,1,0:T(8,128)S(1)}, f32[4,256,256]{2,1,0:T(8,128)}, u32[]{:S(2)}) %copy-start.1) | copy-done | bytes 1048600
  1.2 1.2 %copy-done.3 = f32[4,256,256]{2,1,0:T(8,128)S(1)} copy-done((f32[4,256,256]{2,1,0:T(8,128)S(1)}, f32[4,256,256]{2,1,0:T(8,128)}, u32[]{:S(2)}) %copy-start.3) | copy-done | bytes 1048600
  2.5 1.8 %shard_map.37.mine = f32[2,256,256]{2,1,0:T(8,128)S(1)} custom-call(f32[4,256,256]{2,1,0:T(8,128)S(1)} %copy-done.1, f32[4,256,256]{2,1,0:T(8,128)S(1)} %copy-done.3), custom_call_target="tpu_custom_call" | custom-call | flops 905969664 | bytes 2359296 | tf_op jit(solution)/shard_map/pallas_call | solution.py:132
  4.3 3.3 %collective-permute-start = (f32[2,256,256]{2,1,0:T(8,128)S(1)}, f32[2,256,256]{2,1,0:T(8,128)S(1)}, u32[]{:S(2)}, u32[]{:S(2)}) collective-permute-start(f32[2,256,256]{2,1,0:T(8,128)S(1)} %shard_map.37.mine), channel_id=1, source_target_pairs={{0,1},{1,0},{2,3},{3,2},{4,5},{5,4},{6,7},{7,6},{8,9},{9,8},{10,11... | collective-permute-start | bytes 1572872 | tf_op jit(solution)/shard_map/ppermute | solution.py:157
  7.7 1.5 %collective-permute-done.other = f32[2,256,256]{2,1,0:T(8,128)S(1)} collective-permute-done((f32[2,256,256]{2,1,0:T(8,128)S(1)}, f32[2,256,256]{2,1,0:T(8,128)S(1)}, u32[]{:S(2)}, u32[]{:S(2)}) %collective-permute-start) | collective-permute-done | bytes 524320 | tf_op jit(solution)/shard_map/ppermute | solution.py:157
  9.1 1.3 %shard_map.39 = (f32[2,256,256]{2,1,0:T(8,128)S(1)}, f32[256,256]{1,0:T(8,128)S(1)}) custom-call(s32[2]{0:T(128)S(1)} %pad_add_fusion.7.flags, f32[2,256,256]{2,1,0:T(8,128)S(1)} %shard_map.37.mine, f32[2,256,256]{2,1,0:T(8,128)S(1)} %collective-permute-done.other), custom_call_target="tpu_custom_call" | custom-call | flops 301989888 | bytes 786432 | tf_op jit(solution)/shard_map/pallas_call | solution.py:132
  10.5 7.5 %collective-permute-done.1.near = f32[256,256]{1,0:T(8,128)S(1)} collective-permute-done((f32[256,256]{1,0:T(8,128)S(1)}, f32[256,256]{1,0:T(8,128)S(1)}, u32[]{:S(2)}, u32[]{:S(2)}) %collective-permute-start.1) | collective-permute-done | bytes 262176 | tf_op jit(solution)/shard_map/ppermute | solution.py:157
  18.0 1.2 %collective-permute-start.2 = (f32[256,256]{1,0:T(8,128)S(1)}, f32[256,256]{1,0:T(8,128)S(1)}, u32[]{:S(2)}, u32[]{:S(2)}) collective-permute-start(f32[256,256]{1,0:T(8,128)S(1)} %collective-permute-done.1.near), channel_id=1, source_target_pairs={{0,1},{1,0},{2,3},{3,2},{4,5},{5,4},{6,7},{7,6},{8,9},{9,8},{10,11... | collective-permute-start | bytes 786440 | tf_op jit(solution)/shard_map/ppermute | solution.py:157
  20.4 1.3 %shard_map.41 = (f32[2,256,256]{2,1,0:T(8,128)S(1)}, f32[256,256]{1,0:T(8,128)S(1)}) custom-call(s32[2]{0:T(128)S(1)} %pad_add_fusion.6.flags, f32[2,256,256]{2,1,0:T(8,128)S(1)} %get-tuple-element.20.mine, f32[256,256]{1,0:T(8,128)S(1)} %collective-permute-done.1.near, f32[256,256]{1,0:T(8,128)S(1)} %collective-permute-done.2.far), custom_call_target="tpu_custom_call" | custom-call | flops 301989888 | bytes 786432 | tf_op jit(solution)/shard_map/pallas_call | solution.py:132
  21.7 1.3 %collective-permute-start.3 = (f32[256,256]{1,0:T(8,128)S(1)}, f32[256,256]{1,0:T(8,128)S(1)}, u32[]{:S(2)}, u32[]{:S(2)}) collective-permute-start(f32[256,256]{1,0:T(8,128)S(1)} %get-tuple-element.21), channel_id=1, source_target_pairs={{0,4},{1,5},{2,6},{3,7},{4,0},{5,1},{6,2},{7,3},{8,12},{9,13},{10,... | collective-permute-start | bytes 786440 | tf_op jit(solution)/shard_map/ppermute | solution.py:157
  23.0 7.8 %collective-permute-done.3.near = f32[256,256]{1,0:T(8,128)S(1)} collective-permute-done((f32[256,256]{1,0:T(8,128)S(1)}, f32[256,256]{1,0:T(8,128)S(1)}, u32[]{:S(2)}, u32[]{:S(2)}) %collective-permute-start.3) | collective-permute-done | bytes 262176 | tf_op jit(solution)/shard_map/ppermute | solution.py:157
  33.2 1.3 %shard_map.43 = (f32[2,256,256]{2,1,0:T(8,128)S(1)}, f32[256,256]{1,0:T(8,128)S(1)}) custom-call(s32[2]{0:T(128)S(1)} %pad_add_fusion.5.flags, f32[2,256,256]{2,1,0:T(8,128)S(1)} %get-tuple-element.22.mine, f32[256,256]{1,0:T(8,128)S(1)} %collective-permute-done.3.near, f32[256,256]{1,0:T(8,128)S(1)} %collective-permute-done.4.far), custom_call_target="tpu_custom_call" | custom-call | flops 301989888 | bytes 786432 | tf_op jit(solution)/shard_map/pallas_call | solution.py:132
  34.6 7.5 %collective-permute-done.5.near = f32[256,256]{1,0:T(8,128)S(1)} collective-permute-done((f32[256,256]{1,0:T(8,128)S(1)}, f32[256,256]{1,0:T(8,128)S(1)}, u32[]{:S(2)}, u32[]{:S(2)}) %collective-permute-start.5) | collective-permute-done | bytes 262176 | tf_op jit(solution)/shard_map/ppermute | solution.py:157
  44.5 1.3 %shard_map.45 = (f32[2,256,256]{2,1,0:T(8,128)S(1)}, f32[256,256]{1,0:T(8,128)S(1)}) custom-call(s32[2]{0:T(128)S(1)} %pad_add_fusion.4.flags, f32[2,256,256]{2,1,0:T(8,128)S(1)} %get-tuple-element.24.mine, f32[256,256]{1,0:T(8,128)S(1)} %collective-permute-done.5.near, f32[256,256]{1,0:T(8,128)S(1)} %collective-permute-done.6.far), custom_call_target="tpu_custom_call" | custom-call | flops 301989888 | bytes 786432 | tf_op jit(solution)/shard_map/pallas_call | solution.py:132
  47.6 8.0 %collective-permute-done.7.near = f32[256,256]{1,0:T(8,128)S(1)} collective-permute-done((f32[256,256]{1,0:T(8,128)S(1)}, f32[256,256]{1,0:T(8,128)S(1)}, u32[]{:S(2)}, u32[]{:S(2)}) %collective-permute-start.7) | collective-permute-done | bytes 262176 | tf_op jit(solution)/shard_map/ppermute | solution.py:157
  59.0 1.3 %shard_map.47 = (f32[2,256,256]{2,1,0:T(8,128)S(1)}, f32[256,256]{1,0:T(8,128)S(1)}) custom-call(s32[2]{0:T(128)S(1)} %pad_add_fusion.3.flags, f32[2,256,256]{2,1,0:T(8,128)S(1)} %copy-done.8, f32[256,256]{1,0:T(8,128)S(1)} %collective-permute-done.7.near, f32[256,256]{1,0:T(8,128)S(1)} %collective-permute-done.8.far), custom_call_target="tpu_custom_call" | custom-call | flops 301989888 | bytes 786432 | tf_op jit(solution)/shard_map/pallas_call | solution.py:132
  61.1 7.5 %collective-permute-done.9.near = f32[256,256]{1,0:T(8,128)S(1)} collective-permute-done((f32[256,256]{1,0:T(8,128)S(1)}, f32[256,256]{1,0:T(8,128)S(1)}, u32[]{:S(2)}, u32[]{:S(2)}) %collective-permute-start.9) | collective-permute-done | bytes 262176 | tf_op jit(solution)/shard_map/ppermute | solution.py:157
  68.6 1.2 %collective-permute-start.10 = (f32[256,256]{1,0:T(8,128)S(1)}, f32[256,256]{1,0:T(8,128)S(1)}, u32[]{:S(2)}, u32[]{:S(2)}) collective-permute-start(f32[256,256]{1,0:T(8,128)S(1)} %collective-permute-done.9.near), channel_id=1, source_target_pairs={{0,1},{1,0},{2,3},{3,2},{4,5},{5,4},{6,7},{7,6},{8,9},{9,8},{10,11... | collective-permute-start | bytes 786440 | tf_op jit(solution)/shard_map/ppermute | solution.py:157
  72.0 1.3 %shard_map.49 = (f32[2,256,256]{2,1,0:T(8,128)S(1)}, f32[256,256]{1,0:T(8,128)S(1)}) custom-call(s32[2]{0:T(128)S(1)} %pad_add_fusion.2.flags, f32[2,256,256]{2,1,0:T(8,128)S(1)} %copy-done.10, f32[256,256]{1,0:T(8,128)S(1)} %collective-permute-done.9.near, f32[256,256]{1,0:T(8,128)S(1)} %collective-permute-done.10.far), custom_call_target="tpu_custom_call" | custom-call | flops 301989888 | bytes 786432 | tf_op jit(solution)/shard_map/pallas_call | solution.py:132
  74.1 1.4 %collective-permute-start.11 = (f32[256,256]{1,0:T(8,128)S(1)}, f32[256,256]{1,0:T(8,128)S(1)}, u32[]{:S(2)}, u32[]{:S(2)}) collective-permute-start(f32[256,256]{1,0:T(8,128)S(1)} %get-tuple-element.29), channel_id=1, source_target_pairs={{0,64},{1,65},{2,66},{3,67},{4,68},{5,69},{6,70},{7,71},{8,72},{9,... | collective-permute-start | bytes 786440 | tf_op jit(solution)/shard_map/ppermute | solution.py:157
  75.6 13.1 %collective-permute-done.11.near = f32[256,256]{1,0:T(8,128)S(1)} collective-permute-done((f32[256,256]{1,0:T(8,128)S(1)}, f32[256,256]{1,0:T(8,128)S(1)}, u32[]{:S(2)}, u32[]{:S(2)}) %collective-permute-start.11) | collective-permute-done | bytes 262176 | tf_op jit(solution)/shard_map/ppermute | solution.py:157
  90.7 2.2 %shard_map.52 = f32[128,256]{1,0:T(8,128)S(1)} custom-call(s32[2]{0:T(128)S(1)} %pad_add_fusion.1.flags, f32[2,256,256]{2,1,0:T(8,128)S(1)} %copy-done.6, f32[256,256]{1,0:T(8,128)S(1)} %collective-permute-done.11.near, f32[256,256]{1,0:T(8,128)} %collective-permute-done.12.far, f32[256,256]{1,0:T(8,128)S(1)} %copy-done), custom_call_target="tpu_custom_call" | custom-call | flops 402653184 | bytes 1048576 | tf_op jit(solution)/shard_map/pallas_call | solution.py:132
  92.9 1.3 %collective-permute-start.13 = (f32[128,256]{1,0:T(8,128)S(1)}, f32[128,256]{1,0:T(8,128)S(1)}, u32[]{:S(2)}, u32[]{:S(2)}) collective-permute-start(f32[128,256]{1,0:T(8,128)S(1)} %shard_map.52), channel_id=1, source_target_pairs={{128,96},{129,97},{130,98},{131,99},{132,100},{133,101},{134,102},... | collective-permute-start | bytes 393224 | tf_op jit(solution)/shard_map/ppermute | solution.py:177
  94.2 1.3 %shard_map.40.before = f32[2,256,256]{2,1,0:T(8,128)S(1)} custom-call(s32[2]{0:T(128)S(1)} %pad_add_fusion.6.flags, f32[2,256,256]{2,1,0:T(8,128)S(1)} %shard_map.38.before, f32[256,256]{1,0:T(8,128)S(1)} %collective-permute-done.1.near, f32[256,256]{1,0:T(8,128)S(1)} %collective-permute-done.2.far), custom_call_target="tpu_custom_call" | custom-call | flops 301989888 | bytes 786432 | tf_op jit(solution)/shard_map/pallas_call | solution.py:132
  95.4 1.3 %shard_map.42.before = f32[2,256,256]{2,1,0:T(8,128)S(1)} custom-call(s32[2]{0:T(128)S(1)} %pad_add_fusion.5.flags, f32[2,256,256]{2,1,0:T(8,128)S(1)} %shard_map.40.before, f32[256,256]{1,0:T(8,128)S(1)} %collective-permute-done.3.near, f32[256,256]{1,0:T(8,128)S(1)} %collective-permute-done.4.far), custom_call_target="tpu_custom_call" | custom-call | flops 301989888 | bytes 786432 | tf_op jit(solution)/shard_map/pallas_call | solution.py:132
  96.7 1.3 %shard_map.44.before = f32[2,256,256]{2,1,0:T(8,128)S(1)} custom-call(s32[2]{0:T(128)S(1)} %pad_add_fusion.4.flags, f32[2,256,256]{2,1,0:T(8,128)S(1)} %shard_map.42.before, f32[256,256]{1,0:T(8,128)S(1)} %collective-permute-done.5.near, f32[256,256]{1,0:T(8,128)S(1)} %collective-permute-done.6.far), custom_call_target="tpu_custom_call" | custom-call | flops 301989888 | bytes 786432 | tf_op jit(solution)/shard_map/pallas_call | solution.py:132
  98.0 1.3 %shard_map.46.before = f32[2,256,256]{2,1,0:T(8,128)S(1)} custom-call(s32[2]{0:T(128)S(1)} %pad_add_fusion.3.flags, f32[2,256,256]{2,1,0:T(8,128)S(1)} %shard_map.44.before, f32[256,256]{1,0:T(8,128)S(1)} %collective-permute-done.7.near, f32[256,256]{1,0:T(8,128)S(1)} %collective-permute-done.8.far), custom_call_target="tpu_custom_call" | custom-call | flops 301989888 | bytes 786432 | tf_op jit(solution)/shard_map/pallas_call | solution.py:132
  99.3 1.3 %shard_map.48.before = f32[2,256,256]{2,1,0:T(8,128)S(1)} custom-call(s32[2]{0:T(128)S(1)} %pad_add_fusion.2.flags, f32[2,256,256]{2,1,0:T(8,128)S(1)} %shard_map.46.before, f32[256,256]{1,0:T(8,128)S(1)} %collective-permute-done.9.near, f32[256,256]{1,0:T(8,128)S(1)} %collective-permute-done.10.far), custom_call_target="tpu_custom_call" | custom-call | flops 301989888 | bytes 786432 | tf_op jit(solution)/shard_map/pallas_call | solution.py:132
  100.6 3.7 %collective-permute-done.13.near = f32[128,256]{1,0:T(8,128)S(1)} collective-permute-done((f32[128,256]{1,0:T(8,128)S(1)}, f32[128,256]{1,0:T(8,128)S(1)}, u32[]{:S(2)}, u32[]{:S(2)}) %collective-permute-start.13) | collective-permute-done | bytes 131104 | tf_op jit(solution)/shard_map/ppermute | solution.py:177
  104.8 1.7 %shard_map.50.suffix = f32[2,256,256]{2,1,0:T(8,128)S(1)} custom-call(s32[2]{0:T(128)S(1)} %pad_add_fusion.1.flags, f32[2,256,256]{2,1,0:T(8,128)S(1)} %shard_map.48.before, f32[256,256]{1,0:T(8,128)S(1)} %collective-permute-done.11.near, f32[256,256]{1,0:T(8,128)} %collective-permute-done.12.far), custom_call_target="tpu_custom_call" | custom-call | flops 301989888 | bytes 786432 | tf_op jit(solution)/shard_map/pallas_call | solution.py:132
  106.6 2.4 %shard_map.51 = (f32[4,256,256]{2,1,0:T(8,128)S(1)}, f32[4,256,256]{2,1,0:T(8,128)S(1)}) custom-call(f32[4,256,256]{2,1,0:T(8,128)S(1)} %copy-done.2, f32[4,256,256]{2,1,0:T(8,128)S(1)} %copy-done.4, f32[2,256,256]{2,1,0:T(8,128)S(1)} %shard_map.50.suffix), custom_call_target="tpu_custom_call" | custom-call | flops 1207959552 | bytes 3145728 | tf_op jit(solution)/shard_map/pallas_call | solution.py:132
  109.0 2.8 %shard_map.53 = f32[4,256,256]{2,1,0:T(8,128)} custom-call(s32[2]{0:T(128)S(1)} %pad_add_fusion.flags, f32[4,256,256]{2,1,0:T(8,128)S(1)} %get-tuple-element.30.gains, f32[4,256,256]{2,1,0:T(8,128)S(1)} %get-tuple-element.31.covs, f32[128,256]{1,0:T(8,128)S(1)} %collective-permute-done.13.near, f32[128,256]{1,0:T(8,128)S(1)} %collective-permute-done.14.far, ...), custom_call_target="tpu_custom_call" | custom-call | flops 805306368 | bytes 2097152 | tf_op jit(solution)/shard_map/pallas_call | solution.py:132
  (45 shorter events, 17.6 us)
Async XLA Ops:
  0.0 1.2 %copy-start.1 = (f32[4,256,256]{2,1,0:T(8,128)S(1)}, f32[4,256,256]{2,1,0:T(8,128)}, u32[]{:S(2)}) copy-start(f32[4,256,256]{2,1,0:T(8,128)} %gains.3) | copy-start | bytes 3145732
  1.2 1.2 %copy-start.3 = (f32[4,256,256]{2,1,0:T(8,128)S(1)}, f32[4,256,256]{2,1,0:T(8,128)}, u32[]{:S(2)}) copy-start(f32[4,256,256]{2,1,0:T(8,128)} %covs.3) | copy-start | bytes 3145732
  4.3 4.9 %collective-permute-start = (f32[2,256,256]{2,1,0:T(8,128)S(1)}, f32[2,256,256]{2,1,0:T(8,128)S(1)}, u32[]{:S(2)}, u32[]{:S(2)}) collective-permute-start(f32[2,256,256]{2,1,0:T(8,128)S(1)} %shard_map.37.mine), channel_id=1, source_target_pairs={{0,1},{1,0},{2,3},{3,2},{4,5},{5,4},{6,7},{7,6},{8,9},{9,8},{10,11... | collective-permute-start | bytes 1572872 | tf_op jit(solution)/shard_map/ppermute | solution.py:157
  10.4 7.6 %collective-permute-start.1 = (f32[256,256]{1,0:T(8,128)S(1)}, f32[256,256]{1,0:T(8,128)S(1)}, u32[]{:S(2)}, u32[]{:S(2)}) collective-permute-start(f32[256,256]{1,0:T(8,128)S(1)} %get-tuple-element.19), channel_id=1, source_target_pairs={{0,2},{1,3},{2,0},{3,1},{4,6},{5,7},{6,4},{7,5},{8,10},{9,11},{10,... | collective-permute-start | bytes 786440 | tf_op jit(solution)/shard_map/ppermute | solution.py:157
  18.0 2.4 %collective-permute-start.2 = (f32[256,256]{1,0:T(8,128)S(1)}, f32[256,256]{1,0:T(8,128)S(1)}, u32[]{:S(2)}, u32[]{:S(2)}) collective-permute-start(f32[256,256]{1,0:T(8,128)S(1)} %collective-permute-done.1.near), channel_id=1, source_target_pairs={{0,1},{1,0},{2,3},{3,2},{4,5},{5,4},{6,7},{7,6},{8,9},{9,8},{10,11... | collective-permute-start | bytes 786440 | tf_op jit(solution)/shard_map/ppermute | solution.py:157
  21.7 9.1 %collective-permute-start.3 = (f32[256,256]{1,0:T(8,128)S(1)}, f32[256,256]{1,0:T(8,128)S(1)}, u32[]{:S(2)}, u32[]{:S(2)}) collective-permute-start(f32[256,256]{1,0:T(8,128)S(1)} %get-tuple-element.21), channel_id=1, source_target_pairs={{0,4},{1,5},{2,6},{3,7},{4,0},{5,1},{6,2},{7,3},{8,12},{9,13},{10,... | collective-permute-start | bytes 786440 | tf_op jit(solution)/shard_map/ppermute | solution.py:157
  30.8 2.4 %collective-permute-start.4 = (f32[256,256]{1,0:T(8,128)S(1)}, f32[256,256]{1,0:T(8,128)S(1)}, u32[]{:S(2)}, u32[]{:S(2)}) collective-permute-start(f32[256,256]{1,0:T(8,128)S(1)} %collective-permute-done.3.near), channel_id=1, source_target_pairs={{0,1},{1,0},{2,3},{3,2},{4,5},{5,4},{6,7},{7,6},{8,9},{9,8},{10,11... | collective-permute-start | bytes 786440 | tf_op jit(solution)/shard_map/ppermute | solution.py:157
  34.5 7.6 %collective-permute-start.5 = (f32[256,256]{1,0:T(8,128)S(1)}, f32[256,256]{1,0:T(8,128)S(1)}, u32[]{:S(2)}, u32[]{:S(2)}) collective-permute-start(f32[256,256]{1,0:T(8,128)S(1)} %get-tuple-element.23), channel_id=1, source_target_pairs={{0,8},{1,9},{2,10},{3,11},{4,12},{5,13},{6,14},{7,15},{8,0},{9,1},... | collective-permute-start | bytes 786440 | tf_op jit(solution)/shard_map/ppermute | solution.py:157
  42.1 2.4 %collective-permute-start.6 = (f32[256,256]{1,0:T(8,128)S(1)}, f32[256,256]{1,0:T(8,128)S(1)}, u32[]{:S(2)}, u32[]{:S(2)}) collective-permute-start(f32[256,256]{1,0:T(8,128)S(1)} %collective-permute-done.5.near), channel_id=1, source_target_pairs={{0,1},{1,0},{2,3},{3,2},{4,5},{5,4},{6,7},{7,6},{8,9},{9,8},{10,11... | collective-permute-start | bytes 786440 | tf_op jit(solution)/shard_map/ppermute | solution.py:157
  45.8 0.8 copy-start.7
  46.6 9.0 %collective-permute-start.7 = (f32[256,256]{1,0:T(8,128)S(1)}, f32[256,256]{1,0:T(8,128)S(1)}, u32[]{:S(2)}, u32[]{:S(2)}) collective-permute-start(f32[256,256]{1,0:T(8,128)S(1)} %get-tuple-element.25), channel_id=1, source_target_pairs={{0,16},{1,17},{2,18},{3,19},{4,20},{5,21},{6,22},{7,23},{8,24},{9,... | collective-permute-start | bytes 786440 | tf_op jit(solution)/shard_map/ppermute | solution.py:157
  55.6 2.4 %collective-permute-start.8 = (f32[256,256]{1,0:T(8,128)S(1)}, f32[256,256]{1,0:T(8,128)S(1)}, u32[]{:S(2)}, u32[]{:S(2)}) collective-permute-start(f32[256,256]{1,0:T(8,128)S(1)} %collective-permute-done.7.near), channel_id=1, source_target_pairs={{0,1},{1,0},{2,3},{3,2},{4,5},{5,4},{6,7},{7,6},{8,9},{9,8},{10,11... | collective-permute-start | bytes 786440 | tf_op jit(solution)/shard_map/ppermute | solution.py:157
  58.0 1.0 copy-start.8
  60.3 0.8 copy-start.9
  61.1 7.5 %collective-permute-start.9 = (f32[256,256]{1,0:T(8,128)S(1)}, f32[256,256]{1,0:T(8,128)S(1)}, u32[]{:S(2)}, u32[]{:S(2)}) collective-permute-start(f32[256,256]{1,0:T(8,128)S(1)} %get-tuple-element.27), channel_id=1, source_target_pairs={{0,32},{1,33},{2,34},{3,35},{4,36},{5,37},{6,38},{7,39},{8,40},{9,... | collective-permute-start | bytes 786440 | tf_op jit(solution)/shard_map/ppermute | solution.py:157
  68.6 2.4 %collective-permute-start.10 = (f32[256,256]{1,0:T(8,128)S(1)}, f32[256,256]{1,0:T(8,128)S(1)}, u32[]{:S(2)}, u32[]{:S(2)}) collective-permute-start(f32[256,256]{1,0:T(8,128)S(1)} %collective-permute-done.9.near), channel_id=1, source_target_pairs={{0,1},{1,0},{2,3},{3,2},{4,5},{5,4},{6,7},{7,6},{8,9},{9,8},{10,11... | collective-permute-start | bytes 786440 | tf_op jit(solution)/shard_map/ppermute | solution.py:157
  71.0 1.0 copy-start.10
  73.3 0.8 copy-start.5
  74.1 14.5 %collective-permute-start.11 = (f32[256,256]{1,0:T(8,128)S(1)}, f32[256,256]{1,0:T(8,128)S(1)}, u32[]{:S(2)}, u32[]{:S(2)}) collective-permute-start(f32[256,256]{1,0:T(8,128)S(1)} %get-tuple-element.29), channel_id=1, source_target_pairs={{0,64},{1,65},{2,66},{3,67},{4,68},{5,69},{6,70},{7,71},{8,72},{9,... | collective-permute-start | bytes 786440 | tf_op jit(solution)/shard_map/ppermute | solution.py:157
  88.6 2.0 %collective-permute-start.12 = (f32[256,256]{1,0:T(8,128)S(1)}, f32[256,256]{1,0:T(8,128)}, u32[]{:S(2)}, u32[]{:S(2)}) collective-permute-start(f32[256,256]{1,0:T(8,128)S(1)} %collective-permute-done.11.near), channel_id=1, source_target_pairs={{0,1},{1,0},{2,3},{3,2},{4,5},{5,4},{6,7},{7,6},{8,9},{9,8},{10,11... | collective-permute-start | bytes 786440 | tf_op jit(solution)/shard_map/ppermute | solution.py:157
  89.5 1.1 %copy-start = (f32[256,256]{1,0:T(8,128)S(1)}, f32[256,256]{1,0:T(8,128)}, u32[]{:S(2)}) copy-start(f32[256,256]{1,0:T(8,128)} %terminal.3) | copy-start | bytes 786436
  89.5 1.1 %copy-start.6 = (f32[2,256,256]{2,1,0:T(8,128)S(1)}, f32[2,256,256]{2,1,0:T(8,128)}, u32[]{:S(2)}) copy-start(f32[2,256,256]{2,1,0:T(8,128)} %copy-done.5) | copy-start | bytes 1572868
  92.9 11.5 %collective-permute-start.13 = (f32[128,256]{1,0:T(8,128)S(1)}, f32[128,256]{1,0:T(8,128)S(1)}, u32[]{:S(2)}, u32[]{:S(2)}) collective-permute-start(f32[128,256]{1,0:T(8,128)S(1)} %shard_map.52), channel_id=1, source_target_pairs={{128,96},{129,97},{130,98},{131,99},{132,100},{133,101},{134,102},... | collective-permute-start | bytes 393224 | tf_op jit(solution)/shard_map/ppermute | solution.py:177
  99.3 7.2 %copy-start.4 = (f32[4,256,256]{2,1,0:T(8,128)S(1)}, f32[4,256,256]{2,1,0:T(8,128)}, u32[]{:S(2)}) copy-start(f32[4,256,256]{2,1,0:T(8,128)} %covs.3) | copy-start | bytes 3145732
  100.6 5.9 %copy-start.2 = (f32[4,256,256]{2,1,0:T(8,128)S(1)}, f32[4,256,256]{2,1,0:T(8,128)}, u32[]{:S(2)}) copy-start(f32[4,256,256]{2,1,0:T(8,128)} %gains.3) | copy-start | bytes 3145732
  104.4 4.6 %collective-permute-start.14 = (f32[128,256]{1,0:T(8,128)S(1)}, f32[128,256]{1,0:T(8,128)S(1)}, u32[]{:S(2)}, u32[]{:S(2)}) collective-permute-start(f32[128,256]{1,0:T(8,128)S(1)} %collective-permute-done.13.near), channel_id=1, source_target_pairs={{0,1},{1,0},{2,3},{3,2},{4,5},{5,4},{6,7},{7,6},{8,9},{9,8},{10,11... | collective-permute-start | bytes 393224 | tf_op jit(solution)/shard_map/ppermute | solution.py:157

commit v2 on v1

v2 whole, which is shorter than its diff:
```python
from functools import partial

import jax
import jax.numpy as jnp
from jax import lax
from jax.experimental import pallas as pl
from jax.experimental.pallas import tpu as pltpu
from jax.sharding import PartitionSpec as P

AXES = ("grp", "nbr")
F32 = jnp.float32
BF16 = jnp.bfloat16
TAIL = 8


def split(a):
    high = a.astype(BF16)
    return high, (a - high.astype(F32)).astype(BF16)


def dot(a, b, transposed):
    dims = (((1,), (1 if transposed else 0,)), ((), ()))
    return lax.dot_general(a, b, dims, preferred_element_type=F32)


def product(a, b, transposed=False):
    (ah, al), (bh, bl) = a, b
    return dot(ah, bh, transposed) + (dot(ah, bl, transposed) + dot(al, bh, transposed))


def apply(pair, state):
    gain = split(pair[0])
    return product(split(product(gain, split(state))), gain, True) + pair[1]


def compose(first, second):
    gain = split(first[0])
    mixed = split(product(gain, split(second[1])))
    return product(gain, split(second[0])), product(mixed, gain, True) + first[1]


def pair_of(ref):
    return ref[0], ref[1]


def put(ref, pair):
    ref[0] = pair[0]
    ref[1] = pair[1]


def choose(flag, a, b):
    return jax.tree.map(lambda x, y: jnp.where(flag, x, y), a, b)


def places(size):
    shape = (size, size)
    return lax.broadcasted_iota(jnp.int32, shape, 0), lax.broadcasted_iota(jnp.int32, shape, 1)


def identity_pair(size):
    rows, cols = places(size)
    return (rows == cols).astype(F32), jnp.zeros((size, size), F32)


def widen(block):
    half = block.shape[0] // 2
    return jnp.concatenate([block[:half], block[half:]], axis=1)


def narrow(rows):
    half = rows.shape[1] // 2
    return jnp.concatenate([rows[:, :half], rows[:, half:]], axis=0)


def pack(core, cov):
    half = cov.shape[0] // 2
    rows, cols = places(half)
    upper, across, lower = cov[:half, :half], cov[:half, half:], cov[half:, half:]
    both = jnp.where(rows >= cols, upper, lower)
    diagonal = jnp.sum(jnp.where(rows == cols, lower, 0.0), axis=0, keepdims=True)
    tail = jnp.broadcast_to(jnp.concatenate([diagonal, diagonal], axis=1), (TAIL, 2 * half))
    return jnp.concatenate([widen(jnp.where(core == 0, both, across)), tail], axis=0)


def unpack(first, second):
    rows_sent = first.shape[0] - TAIL
    both, across = narrow(first[:rows_sent]), narrow(second[:rows_sent])
    diagonal = first[rows_sent : rows_sent + 1, : both.shape[1]]
    rows, cols = places(both.shape[0])
    turned = both.T
    upper = jnp.where(rows >= cols, both, turned)
    lower = jnp.where(rows == cols, diagonal, jnp.where(rows < cols, both, turned))
    return jnp.concatenate(
        [jnp.concatenate([upper, across], axis=1), jnp.concatenate([across.T, lower], axis=1)], axis=0
    )


def message(core, pair):
    half = pair[0].shape[0] // 2
    return jnp.concatenate([jnp.where(core == 0, pair[0][:half], pair[0][half:]), pack(core, pair[1])], axis=0)


def received(core, near, far):
    first, second = choose(core == 0, (near[...], far[...]), (far[...], near[...]))
    half = first.shape[1] // 2
    return jnp.concatenate([first[:half], second[:half]], axis=0), unpack(first[half:], second[half:])


def local_kernel(flags, gains, covs, total, gain_buf, cov_buf, gain_sems, cov_sems):
    count = gain_buf.shape[0]
    copies = {}
    for k in range(0, count, 2):
        for name, at in (("g", k), ("c", k + 1), ("g", k + 1), ("c", k)):
            if at < count:
                source, buf, sems = (gains, gain_buf, gain_sems) if name == "g" else (covs, cov_buf, cov_sems)
                copies[name, at] = pltpu.make_async_copy(source.at[at], buf.at[at], sems.at[at])
                copies[name, at].start()
    pairs = []
    for k in range(0, count, 2):
        for at in range(k, min(k + 2, count)):
            copies["g", at].wait()
            copies["c", at].wait()
        now = [(gain_buf[at], cov_buf[at]) for at in range(k, min(k + 2, count))]
        pairs.append(compose(*now) if len(now) == 2 else now[0])
    while len(pairs) > 1:
        pairs = [compose(*pairs[i : i + 2]) if i + 1 < len(pairs) else pairs[i] for i in range(0, len(pairs), 2)]
    put(total, pairs[0])


def first_kernel(flags, mine, other, total, send):
    later = flags[0] != 0
    near, far = pair_of(mine), pair_of(other)
    new = compose(choose(later, far, near), choose(later, near, far))
    put(total, new)
    send[...] = message(flags[0], new)


def four_kernel(flags, mine, near, far, before, group, total, send, *, axis):
    place = flags[axis]
    rows = near.shape[0] // 3
    group[place] = mine[...]
    for d in range(1, 4):
        part = pl.ds((d - 1) * rows, rows)
        gain, cov = received(flags[0], near.at[part], far.at[part])
        group[place ^ d, 0] = gain
        group[place ^ d, 1] = cov
    first = compose(pair_of(group.at[0]), pair_of(group.at[1]))
    second = compose(pair_of(group.at[2]), pair_of(group.at[3]))
    put(group.at[2], second)
    new = compose(first, second)
    put(total, new)
    send[...] = message(flags[0], new)


def two_kernel(flags, mine, near, far, terminal, before, other, total, send, send_state, *, axis):
    late = received(flags[0], near, far)
    put(other, late)
    own = pair_of(mine)
    later = flags[axis] != 0
    first, second = choose(later, late, own), choose(later, own, late)
    new = compose(first, second)
    put(total, new)
    send[...] = message(flags[0], new)
    send_state[...] = pack(flags[0], apply(first, apply(second, terminal[...])))


def received_state(core, near, far):
    return unpack(*choose(core == 0, (near[...], far[...]), (far[...], near[...])))


def state_kernel(flags, mine, near, far, before, state, send):
    state[...] = received_state(flags[0], near, far)
    send[...] = pack(flags[0], apply(pair_of(mine), state[...]))


def first_suffix_kernel(flags, other, suffix):
    put(suffix, choose(flags[0] != 0, identity_pair(suffix.shape[1]), pair_of(other)))


def four_suffix_kernel(flags, before, group, suffix, *, axis):
    place = flags[axis]
    later = pair_of(group.at[2])
    whole = compose(pair_of(group.at[1]), later)
    step = choose(place == 0, whole, choose(place == 1, later, pair_of(group.at[3])))
    old = pair_of(before)
    put(suffix, choose(place == 3, old, compose(old, step)))


def two_suffix_kernel(flags, before, other, suffix, *, axis):
    old = pair_of(before)
    put(suffix, choose(flags[axis] != 0, old, compose(old, pair_of(other))))


def prepare_kernel(gains, covs, suffix, gain_out, cov_out):
    pair = pair_of(suffix)
    for k in range(gains.shape[0] - 1, -1, -1):
        pair = compose((gains[k], covs[k]), pair)
        gain_out[k] = pair[0]
        cov_out[k] = pair[1]


def final_kernel(flags, gains, covs, near, far, part_near, part_far, upper, terminal, out, buf, sems, *, axis):
    highest, high = flags[axis] != 0, flags[axis - 1] != 0
    low = received_state(flags[0], near, far)
    state = jnp.where(highest, jnp.where(high, terminal[...], upper[...]), low)
    moved = apply(received(flags[0], part_near, part_far), low)
    state = split(jnp.where(jnp.logical_or(highest, high), state, moved))
    copies = []
    for k in range(gains.shape[0]):
        gain = split(gains[k])
        buf[k] = product(split(product(gain, state)), gain, True) + covs[k]
        copies.append(pltpu.make_async_copy(buf.at[k], out.at[k], sems.at[k]))
        copies[-1].start()
    for copy in copies:
        copy.wait()


VMEM, SMEM, HBM = pltpu.VMEM, pltpu.SMEM, pltpu.HBM


def call(kernel, products, outs, args, scratch=()):
    width = outs[0][0][-1]
    placed = [x if space in (SMEM, pl.ANY) else pltpu.with_memory_space_constraint(x, space) for x, space in args]
    return pl.pallas_call(
        kernel,
        out_shape=[space(shape, F32) for shape, space in outs],
        in_specs=[pl.BlockSpec(memory_space=space) for _, space in args],
        out_specs=[pl.BlockSpec(memory_space=space) for _, space in outs],
        scratch_shapes=list(scratch),
        cost_estimate=pl.CostEstimate(
            flops=products * 6 * width**3, transcendentals=0, bytes_accessed=4 * width * width * products
        ),
        compiler_params=pltpu.CompilerParams(vmem_limit_bytes=12 * 2**20),
    )(*placed)


def per_device(gains, covs, terminal):
    count, width, _ = gains.shape
    groups, near_count = lax.axis_size("grp"), lax.axis_size("nbr")
    devices = groups * near_count
    place = lax.axis_index("grp") * near_count + lax.axis_index("nbr")
    bits = [(0, 1), (1, 3), (3, 3), (5, 1), (6, 1), (7, 1)]
    flags = jnp.stack([(place >> at) & mask for at, mask in bits]).astype(jnp.int32), SMEM
    pair, group = (2, width, width), (4, 2, width, width)
    packed = width // 4 + TAIL
    sent = (width // 2 + packed, width)
    stack = (count, width, width)

    def permute(x, pairs):
        return lax.ppermute(x, AXES, pairs)

    def swap(x):
        return permute(x, [(i, i ^ 1) for i in range(devices)])

    def inside(x):
        return x, VMEM

    sems = [pltpu.SemaphoreType.DMA((count,))]
    (total,) = call(
        local_kernel,
        9,
        [(pair, VMEM)],
        [flags, (gains, HBM), (covs, HBM)],
        [VMEM(stack, F32), VMEM(stack, F32)] + sems * 2,
    )
    other = swap(total)
    total, send = call(
        first_kernel, 3, [(pair, VMEM), (sent, VMEM)], [flags, inside(total), inside(other)]
    )
    (suffix,) = call(first_suffix_kernel, 1, [(pair, VMEM)], [flags, inside(other)])
    for axis in (1, 2):
        at = bits[axis][0]
        nears = [permute(send, [(i, i ^ (d << at)) for i in range(devices)]) for d in (1, 2, 3)]
        near = jnp.concatenate(nears, axis=0)
        near, suffix = lax.optimization_barrier((near, suffix))
        found, total, send = call(
            partial(four_kernel, axis=axis),
            9,
            [(group, VMEM), (pair, VMEM), (sent, VMEM)],
            [flags, inside(total), inside(near), inside(swap(near)), (suffix, pl.ANY)],
        )
        (suffix,) = call(
            partial(four_suffix_kernel, axis=axis), 6, [(pair, VMEM)], [flags, inside(suffix), inside(found)]
        )
    near = permute(send, [(i, i ^ 32) for i in range(devices)])
    near, suffix = lax.optimization_barrier((near, suffix))
    found, total, send, send_state = call(
        partial(two_kernel, axis=3),
        7,
        [(pair, VMEM), (pair, VMEM), (sent, VMEM), ((packed, width), VMEM)],
        [flags, inside(total), inside(near), inside(swap(near)), inside(terminal), (suffix, pl.ANY)],
    )
    (suffix,) = call(
        partial(two_suffix_kernel, axis=3), 3, [(pair, VMEM)], [flags, inside(suffix), inside(found)]
    )
    row = devices // 8
    near = permute(send_state, [(i, i - 2 * row) for i in range(6 * row, 8 * row)])
    near, suffix = lax.optimization_barrier((near, suffix))
    part_near = permute(send, [(i, i - 2 * row) for i in range(2 * row, 4 * row)])
    upper, send_state = call(
        state_kernel,
        2,
        [((width, width), VMEM), ((packed, width), VMEM)],
        [flags, inside(total), inside(near), inside(swap(near)), (suffix, pl.ANY)],
    )
    ready, added = call(
        prepare_kernel,
        3 * count,
        [(stack, VMEM), (stack, VMEM)],
        [inside(gains), inside(covs), inside(suffix)],
    )
    near = sum(
        permute(send_state, [((source * row) + i, (target * row) + i) for source, target in moves for i in range(row)])
        for moves in (((4, 3), (5, 2)), ((4, 1), (5, 0)))
    )
    near, part_near, ready, added = lax.optimization_barrier((near, part_near, ready, added))
    (out,) = call(
        partial(final_kernel, axis=5),
        2 * count,
        [(stack, HBM)],
        [
            flags,
            inside(ready),
            inside(added),
            inside(near),
            inside(swap(near)),
            inside(part_near),
            inside(swap(part_near)),
            inside(upper),
            inside(terminal),
        ],
        [VMEM(stack, F32)] + sems,
    )
    return out


def solution(mesh):
    placed = (P(AXES, None, None), P(AXES, None, None), P())
    return jax.shard_map(
        per_device,
        mesh=mesh,
        in_specs=placed,
        out_specs=P(AXES, None, None),
        check_vma=False,
    )
```

time: 112 us -> 82.1 us (0.73)
  the two profiles are of different devices: /device:TPU:1 before, /device:TPU:33 now
where the time goes in v2:
time: 82.1 us; the launch traced here: 81.9 us
  waiting for transfers between devices  39 us (48%)
  Pallas kernels  23.6 us (29%)
  starting transfers between devices  18.9 us (23%)
    ppermute x18, waiting for transfers between devices, permute(): return lax.ppermute(x, AXES, pairs)  39 us
    pallas_call x12, Pallas kernels, call(): pl.pallas_call(kernel, out_shape=[space(shape, F32) for shape, space in o...  23.6 us
    ppermute x18, starting transfers between devices, permute(): return lax.ppermute(x, AXES, pairs)  18.9 us
  transfers between devices with their start and end apart: 18, of which 11 were waited for; matrix products, arithmetic and copies ran while one was open for 0% of the time, Pallas kernels for 11%

profile of v2, /device:TPU:33, one launch (start us, length us, event | category | flops | bytes accessed | tf_op | source)
XLA Modules:
  0.0 81.9 jit_solution(2180791558332414392)
XLA Ops:
  0.1 3.5 %shard_map.37.mine = f32[2,256,256]{2,1,0:T(8,128)S(1)} custom-call(s32[6]{0:T(128)S(1)} %stack.27.flags, f32[4,256,256]{2,1,0:T(8,128)} %gains.3, f32[4,256,256]{2,1,0:T(8,128)} %covs.3), custom_call_target="tpu_custom_call" | custom-call | flops 905969664 | bytes 2359296 | tf_op jit(solution)/shard_map/pallas_call | solution.py:224
  3.6 0.8 collective-permute-start
  4.4 1.5 %collective-permute-done.other = f32[2,256,256]{2,1,0:T(8,128)S(1)} collective-permute-done((f32[2,256,256]{2,1,0:T(8,128)S(1)}, f32[2,256,256]{2,1,0:T(8,128)S(1)}, u32[]{:S(2)}, u32[]{:S(2)}) %collective-permute-start) | collective-permute-done | bytes 524320 | tf_op jit(solution)/shard_map/ppermute | solution.py:250
  5.9 1.1 %shard_map.38 = (f32[2,256,256]{2,1,0:T(8,128)S(1)}, f32[200,256]{1,0:T(8,128)S(1)}) custom-call(s32[6]{0:T(128)S(1)} %stack.27.flags, f32[2,256,256]{2,1,0:T(8,128)S(1)} %shard_map.37.mine, f32[2,256,256]{2,1,0:T(8,128)S(1)} %collective-permute-done.other), custom_call_target="tpu_custom_call" | custom-call | flops 301989888 | bytes 786432 | tf_op jit(solution)/shard_map/pallas_call | solution.py:224
  7.0 2.8 %collective-permute-start.3 = (f32[200,256]{1,0:T(8,128)S(1)}, f32[200,256]{1,0:T(8,128)S(1)}, u32[]{:S(2)}, u32[]{:S(2)}) collective-permute-start(f32[200,256]{1,0:T(8,128)S(1)} %get-tuple-element.34), channel_id=1, source_target_pairs={{0,6},{1,7},{2,4},{3,5},{4,2},{5,3},{6,0},{7,1},{8,14},{9,15},{10,... | collective-permute-start | bytes 614408 | tf_op jit(solution)/shard_map/ppermute | solution.py:250
  11.1 7.6 %collective-permute-done.3 = f32[200,256]{1,0:T(8,128)S(1)} collective-permute-done((f32[200,256]{1,0:T(8,128)S(1)}, f32[200,256]{1,0:T(8,128)S(1)}, u32[]{:S(2)}, u32[]{:S(2)}) %collective-permute-start.3) | collective-permute-done | bytes 204832 | tf_op jit(solution)/shard_map/ppermute | solution.py:250
  18.7 0.9 %collective-permute-done.1 = f32[200,256]{1,0:T(8,128)S(1)} collective-permute-done((f32[200,256]{1,0:T(8,128)S(1)}, f32[200,256]{1,0:T(8,128)S(1)}, u32[]{:S(2)}, u32[]{:S(2)}) %collective-permute-start.1) | collective-permute-done | bytes 204832 | tf_op jit(solution)/shard_map/ppermute | solution.py:250
  19.7 1.4 %collective-permute-start.4 = (f32[600,256]{1,0:T(8,128)S(1)}, f32[600,256]{1,0:T(8,128)S(1)}, u32[]{:S(2)}, u32[]{:S(2)}) collective-permute-start(f32[600,256]{1,0:T(8,128)S(1)} %pad_maximum_fusion.near), channel_id=1, source_target_pairs={{0,1},{1,0},{2,3},{3,2},{4,5},{5,4},{6,7},{7,6},{8,9},{9,8},{10,11... | collective-permute-start | bytes 1843208 | tf_op jit(solution)/shard_map/ppermute | solution.py:250
  21.1 1.7 %collective-permute-done.4.far = f32[600,256]{1,0:T(8,128)S(1)} collective-permute-done((f32[600,256]{1,0:T(8,128)S(1)}, f32[600,256]{1,0:T(8,128)S(1)}, u32[]{:S(2)}, u32[]{:S(2)}) %collective-permute-start.4) | collective-permute-done | bytes 614432 | tf_op jit(solution)/shard_map/ppermute | solution.py:250
  22.8 2.4 %shard_map.40 = (f32[4,2,256,256]{3,2,1,0:T(8,128)S(1)}, f32[2,256,256]{2,1,0:T(8,128)S(1)}, f32[200,256]{1,0:T(8,128)S(1)}) custom-call(s32[6]{0:T(128)S(1)} %stack.27.flags, f32[2,256,256]{2,1,0:T(8,128)S(1)} %get-tuple-element.33.mine, f32[600,256]{1,0:T(8,128)S(1)} %pad_maximum_fusion.near, f32[600,256]{1,0:T(8,128)S(1)} %collective-permute-done.4.far, ...), custom_call_target="tpu_custom_call" | custom-call | flops 905969664 | bytes 2359296 | tf_op jit(solution)/shard_map/pallas_call | solution.py:224
  25.1 2.6 %collective-permute-start.7 = (f32[200,256]{1,0:T(8,128)S(1)}, f32[200,256]{1,0:T(8,128)S(1)}, u32[]{:S(2)}, u32[]{:S(2)}) collective-permute-start(f32[200,256]{1,0:T(8,128)S(1)} %get-tuple-element.38), channel_id=1, source_target_pairs={{0,24},{1,25},{2,26},{3,27},{4,28},{5,29},{6,30},{7,31},{8,16},{9,... | collective-permute-start | bytes 614408 | tf_op jit(solution)/shard_map/ppermute | solution.py:250
  28.5 1.7 %shard_map.41.before = f32[2,256,256]{2,1,0:T(8,128)S(1)} custom-call(s32[6]{0:T(128)S(1)} %stack.27.flags, f32[2,256,256]{2,1,0:T(8,128)S(1)} %shard_map.39.before, f32[4,2,256,256]{3,2,1,0:T(8,128)S(1)} %get-tuple-element.39.group), custom_call_target="tpu_custom_call" | custom-call | flops 603979776 | bytes 1572864 | tf_op jit(solution)/shard_map/pallas_call | solution.py:224
  30.2 6.6 %collective-permute-done.7 = f32[200,256]{1,0:T(8,128)S(1)} collective-permute-done((f32[200,256]{1,0:T(8,128)S(1)}, f32[200,256]{1,0:T(8,128)S(1)}, u32[]{:S(2)}, u32[]{:S(2)}) %collective-permute-start.7) | collective-permute-done | bytes 204832 | tf_op jit(solution)/shard_map/ppermute | solution.py:250
  37.5 1.6 %collective-permute-start.8 = (f32[600,256]{1,0:T(8,128)S(1)}, f32[600,256]{1,0:T(8,128)S(1)}, u32[]{:S(2)}, u32[]{:S(2)}) collective-permute-start(f32[600,256]{1,0:T(8,128)S(1)} %pad_maximum_fusion.1.near), channel_id=1, source_target_pairs={{0,1},{1,0},{2,3},{3,2},{4,5},{5,4},{6,7},{7,6},{8,9},{9,8},{10,11... | collective-permute-start | bytes 1843208 | tf_op jit(solution)/shard_map/ppermute | solution.py:250
  39.1 1.7 %collective-permute-done.8.far = f32[600,256]{1,0:T(8,128)S(1)} collective-permute-done((f32[600,256]{1,0:T(8,128)S(1)}, f32[600,256]{1,0:T(8,128)S(1)}, u32[]{:S(2)}, u32[]{:S(2)}) %collective-permute-start.8) | collective-permute-done | bytes 614432 | tf_op jit(solution)/shard_map/ppermute | solution.py:250
  40.7 2.4 %shard_map.42 = (f32[4,2,256,256]{3,2,1,0:T(8,128)S(1)}, f32[2,256,256]{2,1,0:T(8,128)S(1)}, f32[200,256]{1,0:T(8,128)S(1)}) custom-call(s32[6]{0:T(128)S(1)} %stack.27.flags, f32[2,256,256]{2,1,0:T(8,128)S(1)} %get-tuple-element.37.mine, f32[600,256]{1,0:T(8,128)S(1)} %pad_maximum_fusion.1.near, f32[600,256]{1,0:T(8,128)S(1)} %collective-permute-done.8.far, ...), custom_call_target="tpu_custom_call" | custom-call | flops 905969664 | bytes 2359296 | tf_op jit(solution)/shard_map/pallas_call | solution.py:224
  43.1 1.5 %collective-permute-start.9 = (f32[200,256]{1,0:T(8,128)S(1)}, f32[200,256]{1,0:T(8,128)S(1)}, u32[]{:S(2)}, u32[]{:S(2)}) collective-permute-start(f32[200,256]{1,0:T(8,128)S(1)} %get-tuple-element.43), channel_id=1, source_target_pairs={{0,32},{1,33},{2,34},{3,35},{4,36},{5,37},{6,38},{7,39},{8,40},{9,... | collective-permute-start | bytes 614408 | tf_op jit(solution)/shard_map/ppermute | solution.py:250
  44.6 1.7 %shard_map.43.before = f32[2,256,256]{2,1,0:T(8,128)S(1)} custom-call(s32[6]{0:T(128)S(1)} %stack.27.flags, f32[2,256,256]{2,1,0:T(8,128)S(1)} %shard_map.41.before, f32[4,2,256,256]{3,2,1,0:T(8,128)S(1)} %get-tuple-element.44.group), custom_call_target="tpu_custom_call" | custom-call | flops 603979776 | bytes 1572864 | tf_op jit(solution)/shard_map/pallas_call | solution.py:224
  46.4 3.1 %collective-permute-done.9.near = f32[200,256]{1,0:T(8,128)S(1)} collective-permute-done((f32[200,256]{1,0:T(8,128)S(1)}, f32[200,256]{1,0:T(8,128)S(1)}, u32[]{:S(2)}, u32[]{:S(2)}) %collective-permute-start.9) | collective-permute-done | bytes 204832 | tf_op jit(solution)/shard_map/ppermute | solution.py:250
  49.5 1.2 %collective-permute-start.10 = (f32[200,256]{1,0:T(8,128)S(1)}, f32[200,256]{1,0:T(8,128)S(1)}, u32[]{:S(2)}, u32[]{:S(2)}) collective-permute-start(f32[200,256]{1,0:T(8,128)S(1)} %collective-permute-done.9.near), channel_id=1, source_target_pairs={{0,1},{1,0},{2,3},{3,2},{4,5},{5,4},{6,7},{7,6},{8,9},{9,8},{10,11... | collective-permute-start | bytes 614408 | tf_op jit(solution)/shard_map/ppermute | solution.py:250
  50.7 1.1 %collective-permute-done.10.far = f32[200,256]{1,0:T(8,128)S(1)} collective-permute-done((f32[200,256]{1,0:T(8,128)S(1)}, f32[200,256]{1,0:T(8,128)S(1)}, u32[]{:S(2)}, u32[]{:S(2)}) %collective-permute-start.10) | collective-permute-done | bytes 204832 | tf_op jit(solution)/shard_map/ppermute | solution.py:250
  51.8 2.2 %shard_map.44 = (f32[2,256,256]{2,1,0:T(8,128)S(1)}, f32[2,256,256]{2,1,0:T(8,128)S(1)}, f32[200,256]{1,0:T(8,128)S(1)}, f32[72,256]{1,0:T(8,128)S(1)}) custom-call(s32[6]{0:T(128)S(1)} %stack.27.flags, f32[2,256,256]{2,1,0:T(8,128)S(1)} %get-tuple-element.42.mine, f32[200,256]{1,0:T(8,128)S(1)} %collective-permute-done.9.near, ...), custom_call_target="tpu_custom_call" | custom-call | flops 704643072 | bytes 1835008 | tf_op jit(solution)/shard_map/pallas_call | solution.py:224
  54.0 0.7 collective-permute-start.11
  54.7 1.1 %shard_map.45.before.suffix = f32[2,256,256]{2,1,0:T(8,128)S(1)} custom-call(s32[6]{0:T(128)S(1)} %stack.27.flags, f32[2,256,256]{2,1,0:T(8,128)S(1)} %shard_map.43.before, f32[2,256,256]{2,1,0:T(8,128)S(1)} %get-tuple-element.49.other), custom_call_target="tpu_custom_call" | custom-call | flops 301989888 | bytes 786432 | tf_op jit(solution)/shard_map/pallas_call | solution.py:224
  56.2 1.3 %collective-permute-start.15 = (f32[200,256]{1,0:T(8,128)S(1)}, f32[200,256]{1,0:T(8,128)S(1)}, u32[]{:S(2)}, u32[]{:S(2)}) collective-permute-start(f32[200,256]{1,0:T(8,128)S(1)} %get-tuple-element.53), channel_id=1, source_target_pairs={{64,0},{65,1},{66,2},{67,3},{68,4},{69,5},{70,6},{71,7},{72,8},{73... | collective-permute-start | bytes 614408 | tf_op jit(solution)/shard_map/ppermute | solution.py:250
  57.5 1.3 %shard_map.46 = (f32[256,256]{1,0:T(8,128)S(1)}, f32[72,256]{1,0:T(8,128)S(1)}) custom-call(s32[6]{0:T(128)S(1)} %stack.27.flags, f32[2,256,256]{2,1,0:T(8,128)S(1)} %get-tuple-element.47.mine, f32[72,256]{1,0:T(8,128)S(1)} %collective-permute-done.11.near, f32[72,256]{1,0:T(8,128)S(1)} %collective-permute-done.12.far, ...), custom_call_target="tpu_custom_call" | custom-call | flops 201326592 | bytes 524288 | tf_op jit(solution)/shard_map/pallas_call | solution.py:224
  58.8 1.3 %collective-permute-start.14 = (f32[72,256]{1,0:T(8,128)S(1)}, f32[72,256]{1,0:T(8,128)S(1)}, u32[]{:S(2)}, u32[]{:S(2)}) collective-permute-start(f32[72,256]{1,0:T(8,128)S(1)} %get-tuple-element.52), channel_id=1, source_target_pairs={{128,32},{129,33},{130,34},{131,35},{132,36},{133,37},{134,38},{13... | collective-permute-start | bytes 221192 | tf_op jit(solution)/shard_map/ppermute | solution.py:250
  60.8 2.4 %shard_map.47 = (f32[4,256,256]{2,1,0:T(8,128)S(1)}, f32[4,256,256]{2,1,0:T(8,128)S(1)}) custom-call(f32[4,256,256]{2,1,0:T(8,128)S(1)} %copy-done.1, f32[4,256,256]{2,1,0:T(8,128)S(1)} %copy-done.2, f32[2,256,256]{2,1,0:T(8,128)S(1)} %shard_map.45.before.suffix), custom_call_target="tpu_custom_call" | custom-call | flops 1207959552 | bytes 3145728 | tf_op jit(solution)/shard_map/pallas_call | solution.py:224
  63.2 13.0 %collective-permute-done.14 = f32[72,256]{1,0:T(8,128)S(1)} collective-permute-done((f32[72,256]{1,0:T(8,128)S(1)}, f32[72,256]{1,0:T(8,128)S(1)}, u32[]{:S(2)}, u32[]{:S(2)}) %collective-permute-start.14) | collective-permute-done | bytes 73760 | tf_op jit(solution)/shard_map/ppermute | solution.py:250
  76.2 1.1 %collective-permute-start.17 = (f32[200,256]{1,0:T(8,128)S(1)}, f32[200,256]{1,0:T(8,128)S(1)}, u32[]{:S(2)}, u32[]{:S(2)}) collective-permute-start(f32[200,256]{1,0:T(8,128)S(1)} %collective-permute-done.15.part_near), channel_id=1, source_target_pairs={{0,1},{1,0},{2,3},{3,2},{4,5},{5,4},{6,7},{7,6},{8,9},{9,8},{10,11... | collective-permute-start | bytes 614408 | tf_op jit(solution)/shard_map/ppermute | solution.py:250
  77.4 1.2 %collective-permute-done.16.far = f32[72,256]{1,0:T(8,128)S(1)} collective-permute-done((f32[72,256]{1,0:T(8,128)S(1)}, f32[72,256]{1,0:T(8,128)S(1)}, u32[]{:S(2)}, u32[]{:S(2)}) %collective-permute-start.16) | collective-permute-done | bytes 73760 | tf_op jit(solution)/shard_map/ppermute | solution.py:250
  78.6 3.2 %shard_map.48 = f32[4,256,256]{2,1,0:T(8,128)} custom-call(s32[6]{0:T(128)S(1)} %stack.27.flags, f32[4,256,256]{2,1,0:T(8,128)S(1)} %get-tuple-element.56.gains, f32[4,256,256]{2,1,0:T(8,128)S(1)} %get-tuple-element.57.covs, f32[72,256]{1,0:T(8,128)S(1)} %add.7.near, f32[72,256]{1,0:T(8,128)S(1)} %collective-permute-done.16.far, ...), custom_call_target="tpu_custom_call" | custom-call | flops 805306368 | bytes 2097152 | tf_op jit(solution)/shard_map/pallas_call | solution.py:224
  (26 shorter events, 4.2 us)
Async XLA Ops:
  3.6 2.3 %collective-permute-start = (f32[2,256,256]{2,1,0:T(8,128)S(1)}, f32[2,256,256]{2,1,0:T(8,128)S(1)}, u32[]{:S(2)}, u32[]{:S(2)}) collective-permute-start(f32[2,256,256]{2,1,0:T(8,128)S(1)} %shard_map.37.mine), channel_id=1, source_target_pairs={{0,1},{1,0},{2,3},{3,2},{4,5},{5,4},{6,7},{7,6},{8,9},{9,8},{10,11... | collective-permute-start | bytes 1572872 | tf_op jit(solution)/shard_map/ppermute | solution.py:250
  7.0 11.7 %collective-permute-start.3 = (f32[200,256]{1,0:T(8,128)S(1)}, f32[200,256]{1,0:T(8,128)S(1)}, u32[]{:S(2)}, u32[]{:S(2)}) collective-permute-start(f32[200,256]{1,0:T(8,128)S(1)} %get-tuple-element.34), channel_id=1, source_target_pairs={{0,6},{1,7},{2,4},{3,5},{4,2},{5,3},{6,0},{7,1},{8,14},{9,15},{10,... | collective-permute-start | bytes 614408 | tf_op jit(solution)/shard_map/ppermute | solution.py:250
  9.8 8.9 %collective-permute-start.2 = (f32[200,256]{1,0:T(8,128)S(1)}, f32[200,256]{1,0:T(8,128)S(1)}, u32[]{:S(2)}, u32[]{:S(2)}) collective-permute-start(f32[200,256]{1,0:T(8,128)S(1)} %get-tuple-element.34), channel_id=1, source_target_pairs={{0,4},{1,5},{2,6},{3,7},{4,0},{5,1},{6,2},{7,3},{8,12},{9,13},{10,... | collective-permute-start | bytes 614408 | tf_op jit(solution)/shard_map/ppermute | solution.py:250
  10.2 9.5 %collective-permute-start.1 = (f32[200,256]{1,0:T(8,128)S(1)}, f32[200,256]{1,0:T(8,128)S(1)}, u32[]{:S(2)}, u32[]{:S(2)}) collective-permute-start(f32[200,256]{1,0:T(8,128)S(1)} %get-tuple-element.34), channel_id=1, source_target_pairs={{0,2},{1,3},{2,0},{3,1},{4,6},{5,7},{6,4},{7,5},{8,10},{9,11},{10,... | collective-permute-start | bytes 614408 | tf_op jit(solution)/shard_map/ppermute | solution.py:250
  19.7 3.1 %collective-permute-start.4 = (f32[600,256]{1,0:T(8,128)S(1)}, f32[600,256]{1,0:T(8,128)S(1)}, u32[]{:S(2)}, u32[]{:S(2)}) collective-permute-start(f32[600,256]{1,0:T(8,128)S(1)} %pad_maximum_fusion.near), channel_id=1, source_target_pairs={{0,1},{1,0},{2,3},{3,2},{4,5},{5,4},{6,7},{7,6},{8,9},{9,8},{10,11... | collective-permute-start | bytes 1843208 | tf_op jit(solution)/shard_map/ppermute | solution.py:250
  25.1 11.7 %collective-permute-start.7 = (f32[200,256]{1,0:T(8,128)S(1)}, f32[200,256]{1,0:T(8,128)S(1)}, u32[]{:S(2)}, u32[]{:S(2)}) collective-permute-start(f32[200,256]{1,0:T(8,128)S(1)} %get-tuple-element.38), channel_id=1, source_target_pairs={{0,24},{1,25},{2,26},{3,27},{4,28},{5,29},{6,30},{7,31},{8,16},{9,... | collective-permute-start | bytes 614408 | tf_op jit(solution)/shard_map/ppermute | solution.py:250
  27.7 9.1 %collective-permute-start.6 = (f32[200,256]{1,0:T(8,128)S(1)}, f32[200,256]{1,0:T(8,128)S(1)}, u32[]{:S(2)}, u32[]{:S(2)}) collective-permute-start(f32[200,256]{1,0:T(8,128)S(1)} %get-tuple-element.38), channel_id=1, source_target_pairs={{0,16},{1,17},{2,18},{3,19},{4,20},{5,21},{6,22},{7,23},{8,24},{9,... | collective-permute-start | bytes 614408 | tf_op jit(solution)/shard_map/ppermute | solution.py:250
  28.2 9.3 %collective-permute-start.5 = (f32[200,256]{1,0:T(8,128)S(1)}, f32[200,256]{1,0:T(8,128)S(1)}, u32[]{:S(2)}, u32[]{:S(2)}) collective-permute-start(f32[200,256]{1,0:T(8,128)S(1)} %get-tuple-element.38), channel_id=1, source_target_pairs={{0,8},{1,9},{2,10},{3,11},{4,12},{5,13},{6,14},{7,15},{8,0},{9,1},... | collective-permute-start | bytes 614408 | tf_op jit(solution)/shard_map/ppermute | solution.py:250
  37.5 3.2 %collective-permute-start.8 = (f32[600,256]{1,0:T(8,128)S(1)}, f32[600,256]{1,0:T(8,128)S(1)}, u32[]{:S(2)}, u32[]{:S(2)}) collective-permute-start(f32[600,256]{1,0:T(8,128)S(1)} %pad_maximum_fusion.1.near), channel_id=1, source_target_pairs={{0,1},{1,0},{2,3},{3,2},{4,5},{5,4},{6,7},{7,6},{8,9},{9,8},{10,11... | collective-permute-start | bytes 1843208 | tf_op jit(solution)/shard_map/ppermute | solution.py:250
  43.1 8.7 %copy-start = (f32[256,256]{1,0:T(8,128)S(1)}, f32[256,256]{1,0:T(8,128)}, u32[]{:S(2)}) copy-start(f32[256,256]{1,0:T(8,128)} %terminal.3) | copy-start | bytes 786436
  43.1 6.4 %collective-permute-start.9 = (f32[200,256]{1,0:T(8,128)S(1)}, f32[200,256]{1,0:T(8,128)S(1)}, u32[]{:S(2)}, u32[]{:S(2)}) collective-permute-start(f32[200,256]{1,0:T(8,128)S(1)} %get-tuple-element.43), channel_id=1, source_target_pairs={{0,32},{1,33},{2,34},{3,35},{4,36},{5,37},{6,38},{7,39},{8,40},{9,... | collective-permute-start | bytes 614408 | tf_op jit(solution)/shard_map/ppermute | solution.py:250
  49.5 2.3 %collective-permute-start.10 = (f32[200,256]{1,0:T(8,128)S(1)}, f32[200,256]{1,0:T(8,128)S(1)}, u32[]{:S(2)}, u32[]{:S(2)}) collective-permute-start(f32[200,256]{1,0:T(8,128)S(1)} %collective-permute-done.9.near), channel_id=1, source_target_pairs={{0,1},{1,0},{2,3},{3,2},{4,5},{5,4},{6,7},{7,6},{8,9},{9,8},{10,11... | collective-permute-start | bytes 614408 | tf_op jit(solution)/shard_map/ppermute | solution.py:250
  51.8 9.0 %copy-start.1 = (f32[4,256,256]{2,1,0:T(8,128)S(1)}, f32[4,256,256]{2,1,0:T(8,128)}, u32[]{:S(2)}) copy-start(f32[4,256,256]{2,1,0:T(8,128)} %gains.3) | copy-start | bytes 3145732
  51.8 9.0 %copy-start.2 = (f32[4,256,256]{2,1,0:T(8,128)S(1)}, f32[4,256,256]{2,1,0:T(8,128)}, u32[]{:S(2)}) copy-start(f32[4,256,256]{2,1,0:T(8,128)} %covs.3) | copy-start | bytes 3145732
  54.0 1.8 %collective-permute-start.11 = (f32[72,256]{1,0:T(8,128)S(1)}, f32[72,256]{1,0:T(8,128)S(1)}, u32[]{:S(2)}, u32[]{:S(2)}) collective-permute-start(f32[72,256]{1,0:T(8,128)S(1)} %get-tuple-element.48), channel_id=1, source_target_pairs={{192,128},{193,129},{194,130},{195,131},{196,132},{197,133},{198,1... | collective-permute-start | bytes 221192 | tf_op jit(solution)/shard_map/ppermute | solution.py:250
  55.8 1.7 %collective-permute-start.12 = (f32[72,256]{1,0:T(8,128)S(1)}, f32[72,256]{1,0:T(8,128)S(1)}, u32[]{:S(2)}, u32[]{:S(2)}) collective-permute-start(f32[72,256]{1,0:T(8,128)S(1)} %collective-permute-done.11.near), channel_id=1, source_target_pairs={{0,1},{1,0},{2,3},{3,2},{4,5},{5,4},{6,7},{7,6},{8,9},{9,8},{10,11... | collective-permute-start | bytes 221192 | tf_op jit(solution)/shard_map/ppermute | solution.py:250
  56.2 19.9 %collective-permute-start.15 = (f32[200,256]{1,0:T(8,128)S(1)}, f32[200,256]{1,0:T(8,128)S(1)}, u32[]{:S(2)}, u32[]{:S(2)}) collective-permute-start(f32[200,256]{1,0:T(8,128)S(1)} %get-tuple-element.53), channel_id=1, source_target_pairs={{64,0},{65,1},{66,2},{67,3},{68,4},{69,5},{70,6},{71,7},{72,8},{73... | collective-permute-start | bytes 614408 | tf_op jit(solution)/shard_map/ppermute | solution.py:250
  58.8 17.4 %collective-permute-start.14 = (f32[72,256]{1,0:T(8,128)S(1)}, f32[72,256]{1,0:T(8,128)S(1)}, u32[]{:S(2)}, u32[]{:S(2)}) collective-permute-start(f32[72,256]{1,0:T(8,128)S(1)} %get-tuple-element.52), channel_id=1, source_target_pairs={{128,32},{129,33},{130,34},{131,35},{132,36},{133,37},{134,38},{13... | collective-permute-start | bytes 221192 | tf_op jit(solution)/shard_map/ppermute | solution.py:250
  60.1 16.1 %collective-permute-start.13 = (f32[72,256]{1,0:T(8,128)S(1)}, f32[72,256]{1,0:T(8,128)S(1)}, u32[]{:S(2)}, u32[]{:S(2)}) collective-permute-start(f32[72,256]{1,0:T(8,128)S(1)} %get-tuple-element.52), channel_id=1, source_target_pairs={{128,96},{129,97},{130,98},{131,99},{132,100},{133,101},{134,102},... | collective-permute-start | bytes 221192 | tf_op jit(solution)/shard_map/ppermute | solution.py:250
  76.2 2.4 %collective-permute-start.17 = (f32[200,256]{1,0:T(8,128)S(1)}, f32[200,256]{1,0:T(8,128)S(1)}, u32[]{:S(2)}, u32[]{:S(2)}) collective-permute-start(f32[200,256]{1,0:T(8,128)S(1)} %collective-permute-done.15.part_near), channel_id=1, source_target_pairs={{0,1},{1,0},{2,3},{3,2},{4,5},{5,4},{6,7},{7,6},{8,9},{9,8},{10,11... | collective-permute-start | bytes 614408 | tf_op jit(solution)/shard_map/ppermute | solution.py:250
  77.3 1.3 %collective-permute-start.16 = (f32[72,256]{1,0:T(8,128)S(1)}, f32[72,256]{1,0:T(8,128)S(1)}, u32[]{:S(2)}, u32[]{:S(2)}) collective-permute-start(f32[72,256]{1,0:T(8,128)S(1)} %add.7.near), channel_id=1, source_target_pairs={{0,1},{1,0},{2,3},{3,2},{4,5},{5,4},{6,7},{7,6},{8,9},{9,8},{10,11... | collective-permute-start | bytes 221192 | tf_op jit(solution)/shard_map/ppermute | solution.py:250

commit v3 on v2

--- a/solution.py
+++ b/solution.py
@@ -199,11 +199,14 @@
         cov_out[k] = pair[1]
 
 
-def final_kernel(flags, gains, covs, near, far, part_near, part_far, upper, terminal, out, buf, sems, *, axis):
+def final_kernel(flags, gains, covs, near, far, upper, terminal, out, buf, sems, *, axis):
     highest, high = flags[axis] != 0, flags[axis - 1] != 0
-    low = received_state(flags[0], near, far)
+    packed = gains.shape[1] // 4 + TAIL
+    rows = near.shape[0] - packed
+    part, rest = pl.ds(0, rows), pl.ds(rows, packed)
+    low = received_state(flags[0], near.at[rest], far.at[rest])
     state = jnp.where(highest, jnp.where(high, terminal[...], upper[...]), low)
-    moved = apply(received(flags[0], part_near, part_far), low)
+    moved = apply(received(flags[0], near.at[part], far.at[part]), low)
     state = split(jnp.where(jnp.logical_or(highest, high), state, moved))
     copies = []
     for k in range(gains.shape[0]):
@@ -311,9 +314,9 @@
     )
     near = sum(
         permute(send_state, [((source * row) + i, (target * row) + i) for source, target in moves for i in range(row)])
-        for moves in (((4, 3), (5, 2)), ((4, 1), (5, 0)))
-    )
-    near, part_near, ready, added = lax.optimization_barrier((near, part_near, ready, added))
+        for moves in (((4, 3), (5, 2)), ((4, 0), (5, 1)))
+    )
+    near, ready, added = lax.optimization_barrier((jnp.concatenate([part_near, near], axis=0), ready, added))
     (out,) = call(
         partial(final_kernel, axis=5),
         2 * count,
@@ -324,8 +327,6 @@
             inside(added),
             inside(near),
             inside(swap(near)),
-            inside(part_near),
-            inside(swap(part_near)),
             inside(upper),
             inside(terminal),
         ],

time: 82.1 us -> 82.3 us (level)
  the two profiles are of different devices: /device:TPU:33 before, /device:TPU:1 now
where the time goes in v3:
time: 82.3 us; the launch traced here: 82.2 us
  waiting for transfers between devices  38.3 us (47%)
  Pallas kernels  23.5 us (29%)
  starting transfers between devices  19.8 us (24%)
    ppermute x17, waiting for transfers between devices, permute(): return lax.ppermute(x, AXES, pairs)  38.3 us
    pallas_call x12, Pallas kernels, call(): pl.pallas_call(kernel, out_shape=[space(shape, F32) for shape, space in o...  23.5 us
    ppermute x17, starting transfers between devices, permute(): return lax.ppermute(x, AXES, pairs)  19.8 us
  transfers between devices with their start and end apart: 17, of which 11 were waited for; matrix products, arithmetic and copies ran while one was open for 0% of the time, Pallas kernels for 11%

profile of v3, /device:TPU:1, one launch (start us, length us, event | category | flops | bytes accessed | tf_op | source)
XLA Modules:
  0.0 82.2 jit_solution(7790681076060187776)
XLA Ops:
  0.1 3.5 %shard_map.37.mine = f32[2,256,256]{2,1,0:T(8,128)S(1)} custom-call(s32[6]{0:T(128)S(1)} %stack.27.flags, f32[4,256,256]{2,1,0:T(8,128)} %gains.3, f32[4,256,256]{2,1,0:T(8,128)} %covs.3), custom_call_target="tpu_custom_call" | custom-call | flops 905969664 | bytes 2359296 | tf_op jit(solution)/shard_map/pallas_call | solution.py:227
  3.6 3.3 %collective-permute-start = (f32[2,256,256]{2,1,0:T(8,128)S(1)}, f32[2,256,256]{2,1,0:T(8,128)S(1)}, u32[]{:S(2)}, u32[]{:S(2)}) collective-permute-start(f32[2,256,256]{2,1,0:T(8,128)S(1)} %shard_map.37.mine), channel_id=1, source_target_pairs={{0,1},{1,0},{2,3},{3,2},{4,5},{5,4},{6,7},{7,6},{8,9},{9,8},{10,11... | collective-permute-start | bytes 1572872 | tf_op jit(solution)/shard_map/ppermute | solution.py:253
  6.9 1.5 %collective-permute-done.other = f32[2,256,256]{2,1,0:T(8,128)S(1)} collective-permute-done((f32[2,256,256]{2,1,0:T(8,128)S(1)}, f32[2,256,256]{2,1,0:T(8,128)S(1)}, u32[]{:S(2)}, u32[]{:S(2)}) %collective-permute-start) | collective-permute-done | bytes 524320 | tf_op jit(solution)/shard_map/ppermute | solution.py:253
  8.5 1.1 %shard_map.38 = (f32[2,256,256]{2,1,0:T(8,128)S(1)}, f32[200,256]{1,0:T(8,128)S(1)}) custom-call(s32[6]{0:T(128)S(1)} %stack.27.flags, f32[2,256,256]{2,1,0:T(8,128)S(1)} %shard_map.37.mine, f32[2,256,256]{2,1,0:T(8,128)S(1)} %collective-permute-done.other), custom_call_target="tpu_custom_call" | custom-call | flops 301989888 | bytes 786432 | tf_op jit(solution)/shard_map/pallas_call | solution.py:227
  9.6 1.1 %collective-permute-start.3 = (f32[200,256]{1,0:T(8,128)S(1)}, f32[200,256]{1,0:T(8,128)S(1)}, u32[]{:S(2)}, u32[]{:S(2)}) collective-permute-start(f32[200,256]{1,0:T(8,128)S(1)} %get-tuple-element.33), channel_id=1, source_target_pairs={{0,6},{1,7},{2,4},{3,5},{4,2},{5,3},{6,0},{7,1},{8,14},{9,15},{10,... | collective-permute-start | bytes 614408 | tf_op jit(solution)/shard_map/ppermute | solution.py:253
  11.0 1.9 %collective-permute-start.1 = (f32[200,256]{1,0:T(8,128)S(1)}, f32[200,256]{1,0:T(8,128)S(1)}, u32[]{:S(2)}, u32[]{:S(2)}) collective-permute-start(f32[200,256]{1,0:T(8,128)S(1)} %get-tuple-element.33), channel_id=1, source_target_pairs={{0,2},{1,3},{2,0},{3,1},{4,6},{5,7},{6,4},{7,5},{8,10},{9,11},{10,... | collective-permute-start | bytes 614408 | tf_op jit(solution)/shard_map/ppermute | solution.py:253
  13.5 8.0 %collective-permute-done.3 = f32[200,256]{1,0:T(8,128)S(1)} collective-permute-done((f32[200,256]{1,0:T(8,128)S(1)}, f32[200,256]{1,0:T(8,128)S(1)}, u32[]{:S(2)}, u32[]{:S(2)}) %collective-permute-start.3) | collective-permute-done | bytes 204832 | tf_op jit(solution)/shard_map/ppermute | solution.py:253
  22.0 1.6 %collective-permute-start.4 = (f32[600,256]{1,0:T(8,128)S(1)}, f32[600,256]{1,0:T(8,128)S(1)}, u32[]{:S(2)}, u32[]{:S(2)}) collective-permute-start(f32[600,256]{1,0:T(8,128)S(1)} %pad_maximum_fusion.near), channel_id=1, source_target_pairs={{0,1},{1,0},{2,3},{3,2},{4,5},{5,4},{6,7},{7,6},{8,9},{9,8},{10,11... | collective-permute-start | bytes 1843208 | tf_op jit(solution)/shard_map/ppermute | solution.py:253
  23.5 1.7 %collective-permute-done.4.far = f32[600,256]{1,0:T(8,128)S(1)} collective-permute-done((f32[600,256]{1,0:T(8,128)S(1)}, f32[600,256]{1,0:T(8,128)S(1)}, u32[]{:S(2)}, u32[]{:S(2)}) %collective-permute-start.4) | collective-permute-done | bytes 614432 | tf_op jit(solution)/shard_map/ppermute | solution.py:253
  25.2 2.4 %shard_map.40 = (f32[4,2,256,256]{3,2,1,0:T(8,128)S(1)}, f32[2,256,256]{2,1,0:T(8,128)S(1)}, f32[200,256]{1,0:T(8,128)S(1)}) custom-call(s32[6]{0:T(128)S(1)} %stack.27.flags, f32[2,256,256]{2,1,0:T(8,128)S(1)} %get-tuple-element.32.mine, f32[600,256]{1,0:T(8,128)S(1)} %pad_maximum_fusion.near, f32[600,256]{1,0:T(8,128)S(1)} %collective-permute-done.4.far, ...), custom_call_target="tpu_custom_call" | custom-call | flops 905969664 | bytes 2359296 | tf_op jit(solution)/shard_map/pallas_call | solution.py:227
  27.6 1.0 %collective-permute-start.7 = (f32[200,256]{1,0:T(8,128)S(1)}, f32[200,256]{1,0:T(8,128)S(1)}, u32[]{:S(2)}, u32[]{:S(2)}) collective-permute-start(f32[200,256]{1,0:T(8,128)S(1)} %get-tuple-element.37), channel_id=1, source_target_pairs={{0,24},{1,25},{2,26},{3,27},{4,28},{5,29},{6,30},{7,31},{8,16},{9,... | collective-permute-start | bytes 614408 | tf_op jit(solution)/shard_map/ppermute | solution.py:253
  29.1 1.8 %collective-permute-start.5 = (f32[200,256]{1,0:T(8,128)S(1)}, f32[200,256]{1,0:T(8,128)S(1)}, u32[]{:S(2)}, u32[]{:S(2)}) collective-permute-start(f32[200,256]{1,0:T(8,128)S(1)} %get-tuple-element.37), channel_id=1, source_target_pairs={{0,8},{1,9},{2,10},{3,11},{4,12},{5,13},{6,14},{7,15},{8,0},{9,1},... | collective-permute-start | bytes 614408 | tf_op jit(solution)/shard_map/ppermute | solution.py:253
  30.9 1.7 %shard_map.41.before = f32[2,256,256]{2,1,0:T(8,128)S(1)} custom-call(s32[6]{0:T(128)S(1)} %stack.27.flags, f32[2,256,256]{2,1,0:T(8,128)S(1)} %shard_map.39.before, f32[4,2,256,256]{3,2,1,0:T(8,128)S(1)} %get-tuple-element.38.group), custom_call_target="tpu_custom_call" | custom-call | flops 603979776 | bytes 1572864 | tf_op jit(solution)/shard_map/pallas_call | solution.py:227
  32.6 6.9 %collective-permute-done.7 = f32[200,256]{1,0:T(8,128)S(1)} collective-permute-done((f32[200,256]{1,0:T(8,128)S(1)}, f32[200,256]{1,0:T(8,128)S(1)}, u32[]{:S(2)}, u32[]{:S(2)}) %collective-permute-start.7) | collective-permute-done | bytes 204832 | tf_op jit(solution)/shard_map/ppermute | solution.py:253
  39.9 1.6 %collective-permute-start.8 = (f32[600,256]{1,0:T(8,128)S(1)}, f32[600,256]{1,0:T(8,128)S(1)}, u32[]{:S(2)}, u32[]{:S(2)}) collective-permute-start(f32[600,256]{1,0:T(8,128)S(1)} %pad_maximum_fusion.1.near), channel_id=1, source_target_pairs={{0,1},{1,0},{2,3},{3,2},{4,5},{5,4},{6,7},{7,6},{8,9},{9,8},{10,11... | collective-permute-start | bytes 1843208 | tf_op jit(solution)/shard_map/ppermute | solution.py:253
  41.5 1.7 %collective-permute-done.8.far = f32[600,256]{1,0:T(8,128)S(1)} collective-permute-done((f32[600,256]{1,0:T(8,128)S(1)}, f32[600,256]{1,0:T(8,128)S(1)}, u32[]{:S(2)}, u32[]{:S(2)}) %collective-permute-start.8) | collective-permute-done | bytes 614432 | tf_op jit(solution)/shard_map/ppermute | solution.py:253
  43.2 2.4 %shard_map.42 = (f32[4,2,256,256]{3,2,1,0:T(8,128)S(1)}, f32[2,256,256]{2,1,0:T(8,128)S(1)}, f32[200,256]{1,0:T(8,128)S(1)}) custom-call(s32[6]{0:T(128)S(1)} %stack.27.flags, f32[2,256,256]{2,1,0:T(8,128)S(1)} %get-tuple-element.36.mine, f32[600,256]{1,0:T(8,128)S(1)} %pad_maximum_fusion.1.near, f32[600,256]{1,0:T(8,128)S(1)} %collective-permute-done.8.far, ...), custom_call_target="tpu_custom_call" | custom-call | flops 905969664 | bytes 2359296 | tf_op jit(solution)/shard_map/pallas_call | solution.py:227
  45.7 1.7 %shard_map.43.before = f32[2,256,256]{2,1,0:T(8,128)S(1)} custom-call(s32[6]{0:T(128)S(1)} %stack.27.flags, f32[2,256,256]{2,1,0:T(8,128)S(1)} %shard_map.41.before, f32[4,2,256,256]{3,2,1,0:T(8,128)S(1)} %get-tuple-element.43.group), custom_call_target="tpu_custom_call" | custom-call | flops 603979776 | bytes 1572864 | tf_op jit(solution)/shard_map/pallas_call | solution.py:227
  47.4 4.5 %collective-permute-done.9.near = f32[200,256]{1,0:T(8,128)S(1)} collective-permute-done((f32[200,256]{1,0:T(8,128)S(1)}, f32[200,256]{1,0:T(8,128)S(1)}, u32[]{:S(2)}, u32[]{:S(2)}) %collective-permute-start.9) | collective-permute-done | bytes 204832 | tf_op jit(solution)/shard_map/ppermute | solution.py:253
  51.9 1.2 %collective-permute-start.10 = (f32[200,256]{1,0:T(8,128)S(1)}, f32[200,256]{1,0:T(8,128)S(1)}, u32[]{:S(2)}, u32[]{:S(2)}) collective-permute-start(f32[200,256]{1,0:T(8,128)S(1)} %collective-permute-done.9.near), channel_id=1, source_target_pairs={{0,1},{1,0},{2,3},{3,2},{4,5},{5,4},{6,7},{7,6},{8,9},{9,8},{10,11... | collective-permute-start | bytes 614408 | tf_op jit(solution)/shard_map/ppermute | solution.py:253
  53.1 1.1 %collective-permute-done.10.far = f32[200,256]{1,0:T(8,128)S(1)} collective-permute-done((f32[200,256]{1,0:T(8,128)S(1)}, f32[200,256]{1,0:T(8,128)S(1)}, u32[]{:S(2)}, u32[]{:S(2)}) %collective-permute-start.10) | collective-permute-done | bytes 204832 | tf_op jit(solution)/shard_map/ppermute | solution.py:253
  54.2 2.2 %shard_map.44 = (f32[2,256,256]{2,1,0:T(8,128)S(1)}, f32[2,256,256]{2,1,0:T(8,128)S(1)}, f32[200,256]{1,0:T(8,128)S(1)}, f32[72,256]{1,0:T(8,128)S(1)}) custom-call(s32[6]{0:T(128)S(1)} %stack.27.flags, f32[2,256,256]{2,1,0:T(8,128)S(1)} %get-tuple-element.41.mine, f32[200,256]{1,0:T(8,128)S(1)} %collective-permute-done.9.near, ...), custom_call_target="tpu_custom_call" | custom-call | flops 704643072 | bytes 1835008 | tf_op jit(solution)/shard_map/pallas_call | solution.py:227
  56.4 0.7 collective-permute-start.12
  57.1 1.1 %shard_map.45.before.suffix = f32[2,256,256]{2,1,0:T(8,128)S(1)} custom-call(s32[6]{0:T(128)S(1)} %stack.27.flags, f32[2,256,256]{2,1,0:T(8,128)S(1)} %shard_map.43.before, f32[2,256,256]{2,1,0:T(8,128)S(1)} %get-tuple-element.49.other), custom_call_target="tpu_custom_call" | custom-call | flops 301989888 | bytes 786432 | tf_op jit(solution)/shard_map/pallas_call | solution.py:227
  58.7 1.3 %collective-permute-start.11 = (f32[200,256]{1,0:T(8,128)S(1)}, f32[200,256]{1,0:T(8,128)S(1)}, u32[]{:S(2)}, u32[]{:S(2)}) collective-permute-start(f32[200,256]{1,0:T(8,128)S(1)} %get-tuple-element.46), channel_id=1, source_target_pairs={{64,0},{65,1},{66,2},{67,3},{68,4},{69,5},{70,6},{71,7},{72,8},{73... | collective-permute-start | bytes 614408 | tf_op jit(solution)/shard_map/ppermute | solution.py:253
  60.0 1.3 %shard_map.46 = (f32[256,256]{1,0:T(8,128)S(1)}, f32[72,256]{1,0:T(8,128)S(1)}) custom-call(s32[6]{0:T(128)S(1)} %stack.27.flags, f32[2,256,256]{2,1,0:T(8,128)S(1)} %get-tuple-element.47.mine, f32[72,256]{1,0:T(8,128)S(1)} %collective-permute-done.12.near, f32[72,256]{1,0:T(8,128)S(1)} %collective-permute-done.13.far, ...), custom_call_target="tpu_custom_call" | custom-call | flops 201326592 | bytes 524288 | tf_op jit(solution)/shard_map/pallas_call | solution.py:227
  61.2 1.3 %collective-permute-start.15 = (f32[72,256]{1,0:T(8,128)S(1)}, f32[72,256]{1,0:T(8,128)S(1)}, u32[]{:S(2)}, u32[]{:S(2)}) collective-permute-start(f32[72,256]{1,0:T(8,128)S(1)} %get-tuple-element.52), channel_id=1, source_target_pairs={{128,0},{129,1},{130,2},{131,3},{132,4},{133,5},{134,6},{135,7},{1... | collective-permute-start | bytes 221192 | tf_op jit(solution)/shard_map/ppermute | solution.py:253
  63.2 2.4 %shard_map.47 = (f32[4,256,256]{2,1,0:T(8,128)S(1)}, f32[4,256,256]{2,1,0:T(8,128)S(1)}) custom-call(f32[4,256,256]{2,1,0:T(8,128)S(1)} %copy-done.1, f32[4,256,256]{2,1,0:T(8,128)S(1)} %copy-done.2, f32[2,256,256]{2,1,0:T(8,128)S(1)} %shard_map.45.before.suffix), custom_call_target="tpu_custom_call" | custom-call | flops 1207959552 | bytes 3145728 | tf_op jit(solution)/shard_map/pallas_call | solution.py:227
  65.6 11.0 %collective-permute-done.15 = f32[72,256]{1,0:T(8,128)S(1)} collective-permute-done((f32[72,256]{1,0:T(8,128)S(1)}, f32[72,256]{1,0:T(8,128)S(1)}, u32[]{:S(2)}, u32[]{:S(2)}) %collective-permute-start.15) | collective-permute-done | bytes 73760 | tf_op jit(solution)/shard_map/ppermute | solution.py:253
  76.7 1.0 %collective-permute-start.16 = (f32[272,256]{1,0:T(8,128)S(1)}, f32[272,256]{1,0:T(8,128)S(1)}, u32[]{:S(2)}, u32[]{:S(2)}) collective-permute-start(f32[272,256]{1,0:T(8,128)S(1)} %pad_maximum_fusion.2.near), channel_id=1, source_target_pairs={{0,1},{1,0},{2,3},{3,2},{4,5},{5,4},{6,7},{7,6},{8,9},{9,8},{10,11... | collective-permute-start | bytes 835592 | tf_op jit(solution)/shard_map/ppermute | solution.py:253
  77.6 1.2 %collective-permute-done.16.far = f32[272,256]{1,0:T(8,128)S(1)} collective-permute-done((f32[272,256]{1,0:T(8,128)S(1)}, f32[272,256]{1,0:T(8,128)S(1)}, u32[]{:S(2)}, u32[]{:S(2)}) %collective-permute-start.16) | collective-permute-done | bytes 278560 | tf_op jit(solution)/shard_map/ppermute | solution.py:253
  78.8 3.2 %shard_map.48 = f32[4,256,256]{2,1,0:T(8,128)} custom-call(s32[6]{0:T(128)S(1)} %stack.27.flags, f32[4,256,256]{2,1,0:T(8,128)S(1)} %get-tuple-element.55.gains, f32[4,256,256]{2,1,0:T(8,128)S(1)} %get-tuple-element.56.covs, f32[272,256]{1,0:T(8,128)S(1)} %pad_maximum_fusion.2.near, f32[272,256]{1,0:T(8,128)S(1)} %collective-permute-done.16.far, ...), custom_call_target="tpu_custom_call" | custom-call | flops 805306368 | bytes 2097152 | tf_op jit(solution)/shard_map/pallas_call | solution.py:227
  (25 shorter events, 3.7 us)
Async XLA Ops:
  3.6 4.9 %collective-permute-start = (f32[2,256,256]{2,1,0:T(8,128)S(1)}, f32[2,256,256]{2,1,0:T(8,128)S(1)}, u32[]{:S(2)}, u32[]{:S(2)}) collective-permute-start(f32[2,256,256]{2,1,0:T(8,128)S(1)} %shard_map.37.mine), channel_id=1, source_target_pairs={{0,1},{1,0},{2,3},{3,2},{4,5},{5,4},{6,7},{7,6},{8,9},{9,8},{10,11... | collective-permute-start | bytes 1572872 | tf_op jit(solution)/shard_map/ppermute | solution.py:253
  9.6 12.0 %collective-permute-start.3 = (f32[200,256]{1,0:T(8,128)S(1)}, f32[200,256]{1,0:T(8,128)S(1)}, u32[]{:S(2)}, u32[]{:S(2)}) collective-permute-start(f32[200,256]{1,0:T(8,128)S(1)} %get-tuple-element.33), channel_id=1, source_target_pairs={{0,6},{1,7},{2,4},{3,5},{4,2},{5,3},{6,0},{7,1},{8,14},{9,15},{10,... | collective-permute-start | bytes 614408 | tf_op jit(solution)/shard_map/ppermute | solution.py:253
  10.7 10.9 %collective-permute-start.2 = (f32[200,256]{1,0:T(8,128)S(1)}, f32[200,256]{1,0:T(8,128)S(1)}, u32[]{:S(2)}, u32[]{:S(2)}) collective-permute-start(f32[200,256]{1,0:T(8,128)S(1)} %get-tuple-element.33), channel_id=1, source_target_pairs={{0,4},{1,5},{2,6},{3,7},{4,0},{5,1},{6,2},{7,3},{8,12},{9,13},{10,... | collective-permute-start | bytes 614408 | tf_op jit(solution)/shard_map/ppermute | solution.py:253
  11.0 10.9 %collective-permute-start.1 = (f32[200,256]{1,0:T(8,128)S(1)}, f32[200,256]{1,0:T(8,128)S(1)}, u32[]{:S(2)}, u32[]{:S(2)}) collective-permute-start(f32[200,256]{1,0:T(8,128)S(1)} %get-tuple-element.33), channel_id=1, source_target_pairs={{0,2},{1,3},{2,0},{3,1},{4,6},{5,7},{6,4},{7,5},{8,10},{9,11},{10,... | collective-permute-start | bytes 614408 | tf_op jit(solution)/shard_map/ppermute | solution.py:253
  22.0 3.2 %collective-permute-start.4 = (f32[600,256]{1,0:T(8,128)S(1)}, f32[600,256]{1,0:T(8,128)S(1)}, u32[]{:S(2)}, u32[]{:S(2)}) collective-permute-start(f32[600,256]{1,0:T(8,128)S(1)} %pad_maximum_fusion.near), channel_id=1, source_target_pairs={{0,1},{1,0},{2,3},{3,2},{4,5},{5,4},{6,7},{7,6},{8,9},{9,8},{10,11... | collective-permute-start | bytes 1843208 | tf_op jit(solution)/shard_map/ppermute | solution.py:253
  27.6 12.0 %collective-permute-start.7 = (f32[200,256]{1,0:T(8,128)S(1)}, f32[200,256]{1,0:T(8,128)S(1)}, u32[]{:S(2)}, u32[]{:S(2)}) collective-permute-start(f32[200,256]{1,0:T(8,128)S(1)} %get-tuple-element.37), channel_id=1, source_target_pairs={{0,24},{1,25},{2,26},{3,27},{4,28},{5,29},{6,30},{7,31},{8,16},{9,... | collective-permute-start | bytes 614408 | tf_op jit(solution)/shard_map/ppermute | solution.py:253
  28.5 11.0 %collective-permute-start.6 = (f32[200,256]{1,0:T(8,128)S(1)}, f32[200,256]{1,0:T(8,128)S(1)}, u32[]{:S(2)}, u32[]{:S(2)}) collective-permute-start(f32[200,256]{1,0:T(8,128)S(1)} %get-tuple-element.37), channel_id=1, source_target_pairs={{0,16},{1,17},{2,18},{3,19},{4,20},{5,21},{6,22},{7,23},{8,24},{9,... | collective-permute-start | bytes 614408 | tf_op jit(solution)/shard_map/ppermute | solution.py:253
  29.1 10.8 %collective-permute-start.5 = (f32[200,256]{1,0:T(8,128)S(1)}, f32[200,256]{1,0:T(8,128)S(1)}, u32[]{:S(2)}, u32[]{:S(2)}) collective-permute-start(f32[200,256]{1,0:T(8,128)S(1)} %get-tuple-element.37), channel_id=1, source_target_pairs={{0,8},{1,9},{2,10},{3,11},{4,12},{5,13},{6,14},{7,15},{8,0},{9,1},... | collective-permute-start | bytes 614408 | tf_op jit(solution)/shard_map/ppermute | solution.py:253
  39.9 3.2 %collective-permute-start.8 = (f32[600,256]{1,0:T(8,128)S(1)}, f32[600,256]{1,0:T(8,128)S(1)}, u32[]{:S(2)}, u32[]{:S(2)}) collective-permute-start(f32[600,256]{1,0:T(8,128)S(1)} %pad_maximum_fusion.1.near), channel_id=1, source_target_pairs={{0,1},{1,0},{2,3},{3,2},{4,5},{5,4},{6,7},{7,6},{8,9},{9,8},{10,11... | collective-permute-start | bytes 1843208 | tf_op jit(solution)/shard_map/ppermute | solution.py:253
  45.5 8.7 %copy-start = (f32[256,256]{1,0:T(8,128)S(1)}, f32[256,256]{1,0:T(8,128)}, u32[]{:S(2)}) copy-start(f32[256,256]{1,0:T(8,128)} %terminal.3) | copy-start | bytes 786436
  45.5 6.4 %collective-permute-start.9 = (f32[200,256]{1,0:T(8,128)S(1)}, f32[200,256]{1,0:T(8,128)S(1)}, u32[]{:S(2)}, u32[]{:S(2)}) collective-permute-start(f32[200,256]{1,0:T(8,128)S(1)} %get-tuple-element.42), channel_id=1, source_target_pairs={{0,32},{1,33},{2,34},{3,35},{4,36},{5,37},{6,38},{7,39},{8,40},{9,... | collective-permute-start | bytes 614408 | tf_op jit(solution)/shard_map/ppermute | solution.py:253
  51.9 2.3 %collective-permute-start.10 = (f32[200,256]{1,0:T(8,128)S(1)}, f32[200,256]{1,0:T(8,128)S(1)}, u32[]{:S(2)}, u32[]{:S(2)}) collective-permute-start(f32[200,256]{1,0:T(8,128)S(1)} %collective-permute-done.9.near), channel_id=1, source_target_pairs={{0,1},{1,0},{2,3},{3,2},{4,5},{5,4},{6,7},{7,6},{8,9},{9,8},{10,11... | collective-permute-start | bytes 614408 | tf_op jit(solution)/shard_map/ppermute | solution.py:253
  54.2 9.0 %copy-start.1 = (f32[4,256,256]{2,1,0:T(8,128)S(1)}, f32[4,256,256]{2,1,0:T(8,128)}, u32[]{:S(2)}) copy-start(f32[4,256,256]{2,1,0:T(8,128)} %gains.3) | copy-start | bytes 3145732
  54.2 9.0 %copy-start.2 = (f32[4,256,256]{2,1,0:T(8,128)S(1)}, f32[4,256,256]{2,1,0:T(8,128)}, u32[]{:S(2)}) copy-start(f32[4,256,256]{2,1,0:T(8,128)} %covs.3) | copy-start | bytes 3145732
  56.4 1.8 %collective-permute-start.12 = (f32[72,256]{1,0:T(8,128)S(1)}, f32[72,256]{1,0:T(8,128)S(1)}, u32[]{:S(2)}, u32[]{:S(2)}) collective-permute-start(f32[72,256]{1,0:T(8,128)S(1)} %get-tuple-element.48), channel_id=1, source_target_pairs={{192,128},{193,129},{194,130},{195,131},{196,132},{197,133},{198,1... | collective-permute-start | bytes 221192 | tf_op jit(solution)/shard_map/ppermute | solution.py:253
  58.2 1.8 %collective-permute-start.13 = (f32[72,256]{1,0:T(8,128)S(1)}, f32[72,256]{1,0:T(8,128)S(1)}, u32[]{:S(2)}, u32[]{:S(2)}) collective-permute-start(f32[72,256]{1,0:T(8,128)S(1)} %collective-permute-done.12.near), channel_id=1, source_target_pairs={{0,1},{1,0},{2,3},{3,2},{4,5},{5,4},{6,7},{7,6},{8,9},{9,8},{10,11... | collective-permute-start | bytes 221192 | tf_op jit(solution)/shard_map/ppermute | solution.py:253
  58.7 18.0 %collective-permute-start.11 = (f32[200,256]{1,0:T(8,128)S(1)}, f32[200,256]{1,0:T(8,128)S(1)}, u32[]{:S(2)}, u32[]{:S(2)}) collective-permute-start(f32[200,256]{1,0:T(8,128)S(1)} %get-tuple-element.46), channel_id=1, source_target_pairs={{64,0},{65,1},{66,2},{67,3},{68,4},{69,5},{70,6},{71,7},{72,8},{73... | collective-permute-start | bytes 614408 | tf_op jit(solution)/shard_map/ppermute | solution.py:253
  61.2 15.4 %collective-permute-start.15 = (f32[72,256]{1,0:T(8,128)S(1)}, f32[72,256]{1,0:T(8,128)S(1)}, u32[]{:S(2)}, u32[]{:S(2)}) collective-permute-start(f32[72,256]{1,0:T(8,128)S(1)} %get-tuple-element.52), channel_id=1, source_target_pairs={{128,0},{129,1},{130,2},{131,3},{132,4},{133,5},{134,6},{135,7},{1... | collective-permute-start | bytes 221192 | tf_op jit(solution)/shard_map/ppermute | solution.py:253
  62.5 14.1 %collective-permute-start.14 = (f32[72,256]{1,0:T(8,128)S(1)}, f32[72,256]{1,0:T(8,128)S(1)}, u32[]{:S(2)}, u32[]{:S(2)}) collective-permute-start(f32[72,256]{1,0:T(8,128)S(1)} %get-tuple-element.52), channel_id=1, source_target_pairs={{128,96},{129,97},{130,98},{131,99},{132,100},{133,101},{134,102},... | collective-permute-start | bytes 221192 | tf_op jit(solution)/shard_map/ppermute | solution.py:253
  76.7 2.1 %collective-permute-start.16 = (f32[272,256]{1,0:T(8,128)S(1)}, f32[272,256]{1,0:T(8,128)S(1)}, u32[]{:S(2)}, u32[]{:S(2)}) collective-permute-start(f32[272,256]{1,0:T(8,128)S(1)} %pad_maximum_fusion.2.near), channel_id=1, source_target_pairs={{0,1},{1,0},{2,3},{3,2},{4,5},{5,4},{6,7},{7,6},{8,9},{9,8},{10,11... | collective-permute-start | bytes 835592 | tf_op jit(solution)/shard_map/ppermute | solution.py:253
